TPU v7x, 256 devices: a whole 4x4x8 slice. The times are simulated.
256 devices in a mesh: orb: 64 (over y, x, z_lo, core), grid: 4 (over z_hi).
Axes of the slice: x: 4, y: 4, z: 8 (z_hi: 4, z_lo: 2; z = z_hi * 2 + z_lo), core: 2. Of those that a mesh axis runs over, the one named last changes fastest.
Arguments:
- ground_orbitals: float32 [256, 81000], P('orb'), may hold values from -6 to 6
- occupation_signs: int32 [256], P('orb'), may hold values from -1 to 1, as said below
- response_orbitals: float32 [256, 81000], P(('orb', 'grid')), may hold values from -1.5 to 1.5
- window_offsets: int32 [256, 2], P(('orb', 'grid')), may hold values from 0 to 3
- ground_density: float32 [81000], replicated, may hold values from 0.5 to 4
Outputs:
- response_action: float32 [256, 81000], P(('orb', 'grid'))
Inputs may be any that keep to these rules, and one draw needn't show every extreme that they name: `occupation_signs`: every entry is -1 or +1.
All inputs are finite; a program needn't handle non-finite values.
Results may differ from a plain program's by a relative error of at most 0.0003.
Values sent between devices are 32-bit elements; how exact they have to be, the bound alone decides.
A program may use at most 128 MiB of HBM per device.

v0:
```python
import math
import numpy as np
import ml_dtypes
import jax
import jax.numpy as jnp
from jax import lax
from jax.experimental import pallas as pl
from jax.experimental.pallas import tpu as pltpu
from jax.sharding import PartitionSpec as P

NX, NY, NZ = 30, 45, 60
NB = 4
YP, ZP = 48, 64
XH = NX // 2
XC_COEF = 0.3282
HYBRID = 0.25


def real_basis(n):
    j = np.arange(n)
    rows, waves = [np.ones(n) / math.sqrt(n)], [0]
    for m in range(1, (n - 1) // 2 + 1):
        rows += [math.sqrt(2 / n) * np.cos(2 * np.pi * m * j / n), math.sqrt(2 / n) * np.sin(2 * np.pi * m * j / n)]
        waves += [m, m]
    if n % 2 == 0:
        rows.append(np.cos(np.pi * j) / math.sqrt(n))
        waves.append(n // 2)
    return np.array(rows), np.array(waves)


def padded(matrix, size):
    return np.pad(matrix, ((0, size - matrix.shape[0]), (0, size - matrix.shape[1])))


def hi_lo(matrix):
    hi = matrix.astype(ml_dtypes.bfloat16)
    lo = (matrix - hi.astype(np.float64)).astype(ml_dtypes.bfloat16)
    return np.stack([hi, lo])


def tables():
    ty, my = real_basis(NY)
    tz, mz = real_basis(NZ)
    ty, tz = padded(ty, YP), padded(tz, ZP)
    wy = np.kron(np.eye(5), ty)
    wz = np.kron(np.eye(NB), tz.T)
    y_mats = np.stack([hi_lo(wy), hi_lo(wy.T)])
    z_mats = np.stack([hi_lo(wz), hi_lo(wz.T)])
    mx = np.arange(NX // 2 + 1)
    k2 = lambda m, n: (2 * np.pi * m / (0.5 * n)) ** 2
    squared = k2(mx, NX)[:, None, None] + k2(my, NY)[None, :, None] + k2(mz, NZ)[None, None, :]
    green = 4 * np.pi / (squared + 0.25)
    weight = np.where((mx == 0) | (mx == NX // 2), 1.0, 2.0) / NX
    green = green * weight[:, None, None]
    green = np.pad(green, ((0, 0), (0, YP - NY), (0, ZP - NZ)))
    green = np.concatenate([green, green], -1).astype(np.float32)
    return y_mats, z_mats, green


def split(x):
    hi = x.astype(jnp.bfloat16)
    return hi, (x - hi.astype(jnp.float32)).astype(jnp.bfloat16)


def dot(a, b):
    return lax.dot_general(a, b, (((1,), (0,)), ((), ())), preferred_element_type=jnp.float32)


def times_right(x, mat):
    hi, lo = split(x)
    return dot(hi, mat[0]) + dot(lo, mat[0]) + dot(hi, mat[1])


def times_left(mat, x):
    hi, lo = split(x)
    return dot(mat[0], hi) + dot(mat[0], lo) + dot(mat[1], hi)


def combine(values, factors):
    total = None
    for value, factor in zip(values, factors):
        if abs(factor) < 1e-12:
            continue
        term = value if factor == 1.0 else (-value if factor == -1.0 else value * factor)
        total = term if total is None else total + term
    return total


def cos_(m, j):
    return round(math.cos(math.pi * ((m * j) % 30) / 15), 15)


def sin_(m, j):
    return round(math.sin(math.pi * ((m * j) % 30) / 15), 15)


EVEN, ODD = range(0, 16, 2), range(1, 16, 2)
EVEN_S, ODD_S = range(2, 15, 2), range(1, 14, 2)


def x_solve(p, green):
    e = [p[0]] + [p[j] + p[NX - j] for j in range(1, 15)] + [p[15]]
    o = [None] + [p[j] - p[NX - j] for j in range(1, 15)]
    a = [e[j] + e[15 - j] for j in range(8)]
    b = [e[j] - e[15 - j] for j in range(8)]
    u = [o[j] + o[15 - j] for j in range(1, 8)]
    w = [o[j] - o[15 - j] for j in range(1, 8)]
    ev = {m: combine(a, [cos_(m, j) for j in range(8)]) * green[m] for m in EVEN}
    od = {m: combine(b, [cos_(m, j) for j in range(8)]) * green[m] for m in ODD}
    so = {m: combine(u, [sin_(m, j) for j in range(1, 8)]) * green[m] for m in ODD_S}
    se = {m: combine(w, [sin_(m, j) for j in range(1, 8)]) * green[m] for m in EVEN_S}
    pe = [combine([ev[m] for m in EVEN], [cos_(m, j) for m in EVEN]) for j in range(8)]
    po = [combine([od[m] for m in ODD], [cos_(m, j) for m in ODD]) for j in range(8)]
    su = [combine([so[m] for m in ODD_S], [sin_(m, j) for m in ODD_S]) for j in range(1, 8)]
    sw = [combine([se[m] for m in EVEN_S], [sin_(m, j) for m in EVEN_S]) for j in range(1, 8)]
    even = [None] * 16
    odd = [None] * 16
    for j in range(8):
        even[j], even[15 - j] = pe[j] + po[j], pe[j] - po[j]
    for j in range(1, 8):
        odd[j], odd[15 - j] = su[j - 1] + sw[j - 1], su[j - 1] - sw[j - 1]
    out = [None] * NX
    out[0], out[15] = even[0], even[15]
    for j in range(1, 15):
        out[j], out[NX - j] = even[j] + odd[j], even[j] - odd[j]
    return out


def forward_yz(t, p_buf, g_buf, d_buf, y_ref, z_ref):
    planes = pl.ds(5 * t, 5)
    p = p_buf[planes].reshape(5 * YP, 128)
    turned = pltpu.roll(p, ZP, 1)
    low = lax.broadcasted_iota(jnp.int32, p.shape, 1) < ZP
    for half in range(2):
        both = jnp.where(low, p, turned) if half == 0 else jnp.where(low, turned, p)
        g = g_buf[half, planes].reshape(5 * YP, 256)
        s = times_right(jnp.concatenate([both, both], 1) * g, z_ref[0])
        d_buf[half, planes] = times_left(y_ref[0], s).reshape(5, YP, 256)


def middle_x(yt, d_buf, green_ref):
    rows = pl.ds(pl.multiple_of(8 * yt, 8), 8)
    green = [green_ref[m, rows, :] for m in range(16)]
    for lane in (0, 128):
        lanes = pl.ds(lane, 128)
        out = x_solve([d_buf[x // XH, x % XH, rows, lanes] for x in range(NX)], green)
        for x in range(NX):
            d_buf[x // XH, x % XH, rows, lanes] = out[x]


def inverse_yz(t, g_buf, d_buf, w, y_ref, z_ref):
    planes = pl.ds(5 * t, 5)
    sums = []
    for half in range(2):
        s = times_left(y_ref[1], d_buf[half, planes].reshape(5 * YP, 256))
        v = times_right(s, z_ref[1]) * (g_buf[half, planes].reshape(5 * YP, 256) * w)
        pair = v[:, :128] + v[:, 128:]
        sums.append(pair + pltpu.roll(pair, ZP, 1))
    low = lax.broadcasted_iota(jnp.int32, sums[0].shape, 1) < ZP
    return jnp.where(low, sums[0], sums[1]).reshape(5, YP, 128)


MESH = pl.DeviceIdType.MESH
HALF = 80
PART = 5
PLANE = 16
RING = 8


def device(orb, grid):
    return {"orb": orb, "grid": grid}


def remote(src, dst, sends, arrivals, target):
    return pltpu.make_async_remote_copy(
        src_ref=src, dst_ref=dst, send_sem=sends, recv_sem=arrivals, device_id=target, device_id_type=MESH
    )


def place_response(p_ref, p_buf):
    @pl.loop(0, XH)
    def _(i):
        p_buf[i] = jnp.zeros((YP, 128), jnp.float32)
        for half in range(2):
            p_buf[i, 0:NY, ZP * half:ZP * half + NZ] = p_ref[i + XH * half]


def place_ground(g_ref, g_buf):
    @pl.loop(0, XH)
    def _(i):
        for half in range(2):
            g_buf[half, i] = jnp.zeros((YP, 256), jnp.float32)
            for q in range(NB):
                g_buf[half, i, 0:NY, ZP * q:ZP * q + NZ] = g_ref[q, i + XH * half]


def kernel(
    g_ref, p_ref, term_ref, signs_ref, offsets_ref, y_ref, z_ref, green_ref,
    e_ref, rho_ref,
    g_buf, p_buf, q_buf, d_own, d_far, e_out, e_in, pair_in, half_sum, plane_in, part_sum, ring_in, part_all,
    p_sems, e_send, e_recv, pair_sems, swap_sems, plane_send, plane_recv, ring_send, ring_recv, all_send, all_recv,
):
    orb, grid = lax.axis_index("orb"), lax.axis_index("grid")
    core = lax.rem(orb, 2)
    z_lo = lax.rem(orb // 2, 2)
    spot = orb // 4
    level = grid * 2 + z_lo
    left = device(lax.rem(orb + 63, 64), grid)
    right = device(lax.rem(orb + 1, 64), grid)
    partner = device(orb + 1 - 2 * core, grid)

    def in_plane(d):
        other = lax.rem(spot + d, PLANE)
        return other, device(other * 4 + lax.rem(orb, 4), grid)

    def in_ring(d):
        other = lax.rem(level + d, RING)
        return device(spot * 4 + lax.rem(other, 2) * 2 + core, other // 2)

    barrier = pltpu.get_barrier_semaphore()

    def greet(target):
        pl.semaphore_signal(barrier, inc=1, device_id=target, device_id_type=MESH)

    for target in (left, right, partner):
        greet(target)

    @pl.loop(1, PLANE)
    def _(d):
        greet(in_plane(d)[1])

    @pl.loop(1, RING)
    def _(d):
        greet(in_ring(d))

    place_response(p_ref, p_buf)
    p_buf[0, NY:YP, :] = jnp.broadcast_to(offsets_ref[1:2, :], (YP - NY, 128))
    pl.semaphore_wait(barrier, 3 + PLANE - 1 + RING - 1)

    give_p = remote(p_buf, q_buf, p_sems.at[0], p_sems.at[1], left)
    give_p.start()
    give_half = remote(term_ref.at[pl.ds((1 - core) * HALF, HALF)], pair_in, pair_sems.at[0], pair_sems.at[1], partner)
    give_half.start()
    place_ground(g_ref, g_buf)
    give_half.wait()
    half_sum[...] = term_ref[pl.ds(core * HALF, HALF)] + pair_in[...]

    def plane_copy(d):
        other, target = in_plane(d)
        return remote(half_sum.at[pl.ds(other * PART, PART)], plane_in.at[d - 1], plane_send.at[d - 1], plane_recv.at[d - 1], target)

    @pl.loop(1, PLANE)
    def _(d):
        plane_copy(d).start()

    signs = signs_ref[...]
    lane_q = (lax.broadcasted_iota(jnp.int32, (1, 256), 1) // ZP).astype(jnp.float32)

    @pl.loop(0, 3)
    def _(t):
        forward_yz(t, p_buf, g_buf, d_own, y_ref, z_ref)

    @pl.loop(1, PLANE)
    def _(d):
        plane_copy(d).wait()

    part = half_sum[pl.ds(spot * PART, PART)]
    for d in range(PLANE - 1):
        part = part + plane_in[d]
    part_sum[...] = part

    def ring_copy(d):
        return remote(part_sum, ring_in.at[d - 1], ring_send.at[d - 1], ring_recv.at[d - 1], in_ring(d))

    @pl.loop(1, RING)
    def _(d):
        ring_copy(d).start()

    give_p.wait_recv()

    @pl.loop(0, 3)
    def _(t):
        forward_yz(t, q_buf, g_buf, d_far, y_ref, z_ref)

    @pl.loop(1, RING)
    def _(d):
        ring_copy(d).wait()

    part = part_sum[...]
    for d in range(RING - 1):
        part = part + ring_in[d]
    part_all[...] = part
    mine = pl.ds(core * HALF + spot * PART, PART)
    rho_ref[mine] = part

    def all_copy(d):
        return remote(part_all, rho_ref.at[mine], all_send.at[d - 1], all_recv.at[d - 1], in_plane(d)[1])

    @pl.loop(1, PLANE)
    def _(d):
        all_copy(d).start()

    @pl.loop(0, YP // 8)
    def _(yt):
        middle_x(yt, d_far, green_ref)

    @pl.loop(1, PLANE)
    def _(d):
        all_copy(d).wait()

    our_half = rho_ref.at[pl.ds(core * HALF, HALF)]
    swap = remote(our_half, our_half, swap_sems.at[0], swap_sems.at[1], partner)
    swap.start()

    far_offset = q_buf[0, NY:NY + 1, :]
    far_w = signs * (lane_q >= jnp.concatenate([far_offset, far_offset], 1)).astype(jnp.float32)
    own_offset = offsets_ref[0:1, :]
    own_w = signs * (lane_q >= jnp.concatenate([own_offset, own_offset], 1)).astype(jnp.float32)

    def e_copy(t):
        planes = pl.ds(5 * t, 5)
        return remote(e_out.at[planes], e_in.at[planes], e_send.at[t], e_recv.at[t], right)

    @pl.loop(0, 3)
    def _(t):
        e_out[pl.ds(5 * t, 5)] = inverse_yz(t, g_buf, d_far, far_w, y_ref, z_ref)
        e_copy(t).start()

    @pl.loop(0, YP // 8)
    def _(yt):
        middle_x(yt, d_own, green_ref)

    @pl.loop(0, 3)
    def _(t):
        own = inverse_yz(t, g_buf, d_own, own_w, y_ref, z_ref)
        e_copy(t).wait()
        own = own + e_in[pl.ds(5 * t, 5)]
        for i in range(5):
            e_ref[5 * t + i] = own[i, :NY, :NZ]
            e_ref[XH + 5 * t + i] = own[i, :NY, ZP:ZP + NZ]

    give_p.wait_send()
    swap.wait()


def per_device(ground_orbitals, occupation_signs, response_orbitals, window_offsets, ground_density):
    points = response_orbitals.shape[1]
    signs = occupation_signs.astype(jnp.float32)
    own_start = lax.axis_index("grid")
    own_ground = lax.dynamic_slice_in_dim(ground_orbitals, own_start, 1, 0).reshape(points)
    own_sign = lax.dynamic_slice_in_dim(signs, own_start, 1, 0)
    response = response_orbitals.reshape(points)
    term = own_sign * own_ground * response
    term = jnp.pad(term, (0, 2 * HALF * 512 - points)).reshape(2 * HALF, 4, 128)
    signs_lanes = jnp.repeat(signs, ZP)[None]
    offsets = jnp.broadcast_to(window_offsets.astype(jnp.float32).reshape(2, 1), (2, 128))
    y_mats, z_mats, green = tables()
    vmem = pl.BlockSpec(memory_space=pltpu.VMEM)
    f32 = jnp.float32
    dma = pltpu.SemaphoreType.DMA
    exchange, rho = pl.pallas_call(
        kernel,
        out_shape=(
            jax.ShapeDtypeStruct((NX, NY, NZ), f32),
            jax.ShapeDtypeStruct((2 * HALF, 4, 128), f32),
        ),
        in_specs=[vmem] * 8,
        out_specs=(vmem, vmem),
        scratch_shapes=[
            pltpu.VMEM((2, XH, YP, 256), f32),
            pltpu.VMEM((XH, YP, 128), f32),
            pltpu.VMEM((XH, YP, 128), f32),
            pltpu.VMEM((2, XH, YP, 256), f32),
            pltpu.VMEM((2, XH, YP, 256), f32),
            pltpu.VMEM((XH, YP, 128), f32),
            pltpu.VMEM((XH, YP, 128), f32),
            pltpu.VMEM((HALF, 4, 128), f32),
            pltpu.VMEM((HALF, 4, 128), f32),
            pltpu.VMEM((PLANE - 1, PART, 4, 128), f32),
            pltpu.VMEM((PART, 4, 128), f32),
            pltpu.VMEM((RING - 1, PART, 4, 128), f32),
            pltpu.VMEM((PART, 4, 128), f32),
            dma((2,)), dma((3,)), dma((3,)), dma((2,)), dma((2,)),
            dma((PLANE - 1,)), dma((PLANE - 1,)), dma((RING - 1,)), dma((RING - 1,)), dma((PLANE - 1,)), dma((PLANE - 1,)),
        ],
        compiler_params=pltpu.CompilerParams(
            collective_id=0, has_side_effects=True, vmem_limit_bytes=48 << 20
        ),
    )(
        ground_orbitals.reshape(NB, NX, NY, NZ), response.reshape(NX, NY, NZ),
        term, signs_lanes, offsets, y_mats, z_mats, green,
    )
    potential = -XC_COEF * ground_density ** (-2.0 / 3.0) * rho.reshape(-1)[:points]
    return (potential * own_ground - HYBRID * exchange.reshape(points))[None]


def solution(mesh):
    placed = (P("orb", None), P("orb"), P(("orb", "grid"), None), P(("orb", "grid"), None), P())
    return jax.shard_map(
        per_device, mesh=mesh, in_specs=placed, out_specs=P(("orb", "grid"), None), check_vma=False
    )
```

profile of v0, /device:TPU:1, one launch (start us, length us, event | category | flops | bytes accessed | tf_op | source)
XLA Modules:
  0.0 53.7 jit_solution(1358457697145764933)
XLA Ops:
  0.0 0.7 %convert_element_type.8 = f32[4]{0:T(128)S(1)} convert(s32[4]{0:T(128)} %param.9) | non-fusion elementwise | flops 4 | bytes 32 | tf_op jit(solution)/shard_map/convert_element_type | solution.py:348
  0.7 0.6 %dynamic_slice.6 = f32[1]{0:T(128)} dynamic-slice(f32[4]{0:T(128)S(1)} %convert_element_type.8, s32[]{:T(128)S(6)} %select_n.4), dynamic_slice_sizes={1} | dynamic-slice | bytes 12 | tf_op jit(solution)/shard_map/dynamic_slice | solution.py:351
  1.2 0.7 %convert_bitcast_fusion = f32[2]{0:T(128)S(1)} fusion(s32[1,2]{1,0:T(1,128)} %param.11), kind=kLoop, calls=%fused_computation.6 | loop fusion | flops 2 | bytes 16 | tf_op jit(solution)/shard_map/broadcast_in_dim | solution.py:356
  1.9 0.1 broadcast_in_dim.15.offsets_ref
  2.0 0.1 broadcast_in_dim.13
  2.0 0.1 broadcast_in_dim_reshape.3.signs_ref
  2.1 2.3 %dynamic-slice_reduce_fusion = f32[81000]{0:T(1024)S(1)} fusion(f32[4,81000]{1,0:T(4,128)} %param.8, s32[]{:T(128)S(6)} %select_n.4), kind=kLoop, calls=%fused_computation.5 | loop fusion | bytes 648004 | tf_op jit(solution)/shard_map/dynamic_slice | solution.py:350
  4.4 1.8 %reduce = f32[81000]{0:T(1024)S(1)} reduce(f32[1,81000]{1,0:T(1,128)} %param.10, f32[]{:T(128)} %constant.31), dimensions={0}, to_apply=%param.10.reduce_sub_computation | reduce | bytes 648004 | tf_op args[2]
  6.2 0.7 %multiply_multiply_fusion = f32[81000]{0:T(1024)S(1)} fusion(f32[81000]{0:T(1024)S(1)} %reduce, f32[81000]{0:T(1024)S(1)} %dynamic-slice_reduce_fusion, f32[]{:T(128)} %bitcast), kind=kLoop, calls=%fused_computation.4 | loop fusion | flops 162000 | bytes 972004 | tf_op jit(solution)/shard_map/mul | solution.py:353
  6.9 0.5 reshape_reshape.3.p_ref
  7.4 0.0 copy-start
  7.4 0.0 copy-start.1
  7.4 0.0 copy-start.2
  7.5 5.4 %reshape.20.g_ref = f32[4,30,45,60]{3,2,1,0:T(8,128)} reshape(f32[4,81000]{1,0:T(4,128)} %param.8) | data formatting | bytes 2592000 | tf_op jit(solution)/shard_map/reshape | solution.py:390
  12.8 0.0 copy-done
  12.8 0.0 copy-done.1
  12.8 0.0 copy-done.2
  12.8 38.6 %shard_map.82 = (f32[30,45,60]{2,1,0:T(8,128)S(1)}, f32[160,4,128]{2,1,0:T(4,128)S(1)}) custom-call(f32[4,30,45,60]{3,2,1,0:T(8,128)} %reshape.20.g_ref, f32[30,45,60]{2,1,0:T(8,128)S(1)} %reshape_reshape.3.p_ref, f32[160,4,128]{2,1,0:T(4,128)S(1)} %bitcast.5, f32[1,256]{1,0:T(1,128)S(1)} %broadcast_in_dim_reshape.3.signs_ref, ...), custom_call_target="tpu_custom_call" | custom-call | tf_op jit(solution)/shard_map/pallas_call | solution.py:361
  51.4 0.0 copy-start.3
  51.4 0.1 broadcast_multiply_fusion
  51.5 0.5 mul.44
  52.0 0.4 copy-done.3
  52.4 0.4 fusion.1
  52.8 0.9 %broadcast_in_dim.16 = f32[1,81000]{1,0:T(1,128)} reshape(f32[81000]{0:T(1024)S(1)} %fusion.1) | data formatting | bytes 648000 | tf_op jit(solution)/shard_map/broadcast_in_dim | solution.py:394
  (1 shorter events, 0.0 us)
Async XLA Ops:
  7.4 5.4 %copy-start = (bf16[2,2,256,256]{3,2,1,0:T(8,128)(2,1)S(1)}, bf16[2,2,256,256]{3,2,1,0:T(8,128)(2,1)}, u32[]{:S(2)}) copy-start(bf16[2,2,256,256]{3,2,1,0:T(8,128)(2,1)} %constant.23.clone.z_ref) | copy-start | bytes 1572868
  7.4 5.4 %copy-start.1 = (bf16[2,2,240,240]{3,2,1,0:T(8,128)(2,1)S(1)}, bf16[2,2,240,240]{3,2,1,0:T(8,128)(2,1)}, u32[]{:S(2)}) copy-start(bf16[2,2,240,240]{3,2,1,0:T(8,128)(2,1)} %constant.22.clone.y_ref) | copy-start | bytes 1382404
  7.4 5.4 %copy-start.2 = (f32[16,48,128]{2,1,0:T(8,128)S(1)}, f32[16,48,128]{2,1,0:T(8,128)}, u32[]{:S(2)}) copy-start(f32[16,48,128]{2,1,0:T(8,128)} %constant.24.clone.green_ref) | copy-start | bytes 1179652
  51.4 1.0 %copy-start.3 = (f32[81000]{0:T(1024)S(1)}, f32[81000]{0:T(1024)}, u32[]{:S(2)}) copy-start(f32[81000]{0:T(1024)} %param.12) | copy-start | bytes 972004
where the time goes:
time: 54.1 us; the launch traced here: 53.7 us
  Pallas kernels  38.6 us (71%)
  local copies, waits for them, and re-layouts  10.9 us (20%)
  other arithmetic  4.23 us (8%)
    pallas_call x1, Pallas kernels, per_device(): pl.pallas_call(kernel, out_shape=(jax.ShapeDtypeStruct((NX, NY, NZ), f32)...  38.6 us
    reshape x1, local copies, waits for them, and re-layouts, per_device(): ground_orbitals.reshape(NB, NX, NY, NZ)  5.38 us
    dynamic_slice x1, local copies, waits for them, and re-layouts, per_device(): lax.dynamic_slice_in_dim(ground_orbitals, own_start, 1, 0).reshape(points)  2.25 us
    unnamed x1, other arithmetic  1.79 us

commit v1 on v0

--- a/solution.py
+++ b/solution.py
@@ -76,54 +76,71 @@
     return dot(mat[0], hi) + dot(mat[0], lo) + dot(mat[1], hi)
 
 
-def combine(values, factors):
-    total = None
-    for value, factor in zip(values, factors):
-        if abs(factor) < 1e-12:
-            continue
-        term = value if factor == 1.0 else (-value if factor == -1.0 else value * factor)
-        total = term if total is None else total + term
-    return total
-
-
-def cos_(m, j):
-    return round(math.cos(math.pi * ((m * j) % 30) / 15), 15)
-
-
-def sin_(m, j):
-    return round(math.sin(math.pi * ((m * j) % 30) / 15), 15)
-
-
-EVEN, ODD = range(0, 16, 2), range(1, 16, 2)
-EVEN_S, ODD_S = range(2, 15, 2), range(1, 14, 2)
+C3, S3 = 0.5, math.sqrt(3) / 2
+S5A, S5B, R5 = math.sin(2 * math.pi / 5), math.sin(4 * math.pi / 5), math.sqrt(5) / 4
+
+
+def five_even(zero, one, two):
+    total, apart = one + two, (one - two) * R5
+    base = zero - total * 0.25
+    return zero + total, base + apart, base - apart
+
+
+def five_odd(one, two):
+    return one * S5A + two * S5B, one * S5B - two * S5A
+
+
+def five_waves(p):
+    return five_even(p[0], p[1] + p[4], p[2] + p[3]) + five_odd(p[1] - p[4], p[2] - p[3])
+
+
+def five_points(c):
+    zero, one, two = five_even(*c[:3])
+    up, down = five_odd(*c[3:])
+    return [zero, one + up, two + down, two - down, one - up]
+
+
+def wave_of(two, three, five):
+    wave = next(m for m in range(NX) if (m % 2, m % 3, m % 5) == (two, three, five % 5))
+    return min(wave, NX - wave)
 
 
 def x_solve(p, green):
-    e = [p[0]] + [p[j] + p[NX - j] for j in range(1, 15)] + [p[15]]
-    o = [None] + [p[j] - p[NX - j] for j in range(1, 15)]
-    a = [e[j] + e[15 - j] for j in range(8)]
-    b = [e[j] - e[15 - j] for j in range(8)]
-    u = [o[j] + o[15 - j] for j in range(1, 8)]
-    w = [o[j] - o[15 - j] for j in range(1, 8)]
-    ev = {m: combine(a, [cos_(m, j) for j in range(8)]) * green[m] for m in EVEN}
-    od = {m: combine(b, [cos_(m, j) for j in range(8)]) * green[m] for m in ODD}
-    so = {m: combine(u, [sin_(m, j) for j in range(1, 8)]) * green[m] for m in ODD_S}
-    se = {m: combine(w, [sin_(m, j) for j in range(1, 8)]) * green[m] for m in EVEN_S}
-    pe = [combine([ev[m] for m in EVEN], [cos_(m, j) for m in EVEN]) for j in range(8)]
-    po = [combine([od[m] for m in ODD], [cos_(m, j) for m in ODD]) for j in range(8)]
-    su = [combine([so[m] for m in ODD_S], [sin_(m, j) for m in ODD_S]) for j in range(1, 8)]
-    sw = [combine([se[m] for m in EVEN_S], [sin_(m, j) for m in EVEN_S]) for j in range(1, 8)]
-    even = [None] * 16
-    odd = [None] * 16
-    for j in range(8):
-        even[j], even[15 - j] = pe[j] + po[j], pe[j] - po[j]
-    for j in range(1, 8):
-        odd[j], odd[15 - j] = su[j - 1] + sw[j - 1], su[j - 1] - sw[j - 1]
+    grid = [[[p[(15 * a + 10 * b + 6 * c) % NX] for c in range(5)] for b in range(3)] for a in range(2)]
+    back = []
+    for two in range(2):
+        rows = [[grid[0][b][c] - grid[1][b][c] if two else grid[0][b][c] + grid[1][b][c] for c in range(5)] for b in range(3)]
+        both = [rows[1][c] + rows[2][c] for c in range(5)]
+        flat = five_waves([rows[0][c] + both[c] for c in range(5)])
+        cosine = five_waves([rows[0][c] - both[c] * C3 for c in range(5)])
+        sine = five_waves([(rows[1][c] - rows[2][c]) * S3 for c in range(5)])
+        k = lambda three, five: green[wave_of(two, three, five)]
+        flat = [flat[0] * k(0, 0), flat[1] * k(0, 1), flat[2] * k(0, 2), flat[3] * k(0, 1), flat[4] * k(0, 2)]
+        new_c, new_s = [cosine[0] * k(1, 0)] + [None] * 4, [sine[0] * k(1, 0)] + [None] * 4
+        for five in (1, 2):
+            cc, cs, sc, ss = cosine[five], cosine[five + 2], sine[five], sine[five + 2]
+            x_up, x_down = (cc - ss) * k(1, five), (cc + ss) * k(1, -five)
+            y_up, y_down = (sc + cs) * k(1, five), (sc - cs) * k(1, -five)
+            new_c[five], new_s[five + 2] = x_up + x_down, x_down - x_up
+            new_s[five], new_c[five + 2] = y_up + y_down, y_up - y_down
+        flat, cosine, sine = five_points(flat), five_points(new_c), five_points(new_s)
+        lines = [[flat[c] + cosine[c] for c in range(5)], [], []]
+        for c in range(5):
+            middle, side = flat[c] - cosine[c] * C3, sine[c] * S3
+            lines[1].append(middle + side)
+            lines[2].append(middle - side)
+        back.append(lines)
     out = [None] * NX
-    out[0], out[15] = even[0], even[15]
-    for j in range(1, 15):
-        out[j], out[NX - j] = even[j] + odd[j], even[j] - odd[j]
+    for a in range(2):
+        for b in range(3):
+            for c in range(5):
+                plus, minus = back[0][b][c], back[1][b][c]
+                out[(15 * a + 10 * b + 6 * c) % NX] = minus_or(plus, minus, a)
     return out
+
+
+def minus_or(plus, minus, a):
+    return plus - minus if a else plus + minus
 
 
 def forward_yz(t, p_buf, g_buf, d_buf, y_ref, z_ref):
@@ -175,6 +192,10 @@
     return pltpu.make_async_remote_copy(
         src_ref=src, dst_ref=dst, send_sem=sends, recv_sem=arrivals, device_id=target, device_id_type=MESH
     )
+
+
+def drain(ref, sem):
+    pltpu.make_async_copy(ref, ref, sem).wait()
 
 
 def place_response(p_ref, p_buf):
@@ -247,7 +268,7 @@
 
     def plane_copy(d):
         other, target = in_plane(d)
-        return remote(half_sum.at[pl.ds(other * PART, PART)], plane_in.at[d - 1], plane_send.at[d - 1], plane_recv.at[d - 1], target)
+        return remote(half_sum.at[pl.ds(other * PART, PART)], plane_in.at[d - 1], plane_send, plane_recv, target)
 
     @pl.loop(1, PLANE)
     def _(d):
@@ -256,13 +277,11 @@
     signs = signs_ref[...]
     lane_q = (lax.broadcasted_iota(jnp.int32, (1, 256), 1) // ZP).astype(jnp.float32)
 
-    @pl.loop(0, 3)
-    def _(t):
+    for t in range(3):
         forward_yz(t, p_buf, g_buf, d_own, y_ref, z_ref)
 
-    @pl.loop(1, PLANE)
-    def _(d):
-        plane_copy(d).wait()
+    drain(half_sum.at[pl.ds(0, HALF - PART)], plane_send)
+    drain(plane_in, plane_recv)
 
     part = half_sum[pl.ds(spot * PART, PART)]
     for d in range(PLANE - 1):
@@ -270,7 +289,7 @@
     part_sum[...] = part
 
     def ring_copy(d):
-        return remote(part_sum, ring_in.at[d - 1], ring_send.at[d - 1], ring_recv.at[d - 1], in_ring(d))
+        return remote(part_sum, ring_in.at[d - 1], ring_send, ring_recv, in_ring(d))
 
     @pl.loop(1, RING)
     def _(d):
@@ -278,13 +297,11 @@
 
     give_p.wait_recv()
 
-    @pl.loop(0, 3)
-    def _(t):
+    for t in range(3):
         forward_yz(t, q_buf, g_buf, d_far, y_ref, z_ref)
 
-    @pl.loop(1, RING)
-    def _(d):
-        ring_copy(d).wait()
+    drain(ring_in, ring_send)
+    drain(ring_in, ring_recv)
 
     part = part_sum[...]
     for d in range(RING - 1):
@@ -294,7 +311,7 @@
     rho_ref[mine] = part
 
     def all_copy(d):
-        return remote(part_all, rho_ref.at[mine], all_send.at[d - 1], all_recv.at[d - 1], in_plane(d)[1])
+        return remote(part_all, rho_ref.at[mine], all_send, all_recv, in_plane(d)[1])
 
     @pl.loop(1, PLANE)
     def _(d):
@@ -304,9 +321,8 @@
     def _(yt):
         middle_x(yt, d_far, green_ref)
 
-    @pl.loop(1, PLANE)
-    def _(d):
-        all_copy(d).wait()
+    drain(half_sum.at[pl.ds(0, HALF - PART)], all_send)
+    drain(half_sum.at[pl.ds(0, HALF - PART)], all_recv)
 
     our_half = rho_ref.at[pl.ds(core * HALF, HALF)]
     swap = remote(our_half, our_half, swap_sems.at[0], swap_sems.at[1], partner)
@@ -321,8 +337,7 @@
         planes = pl.ds(5 * t, 5)
         return remote(e_out.at[planes], e_in.at[planes], e_send.at[t], e_recv.at[t], right)
 
-    @pl.loop(0, 3)
-    def _(t):
+    for t in range(3):
         e_out[pl.ds(5 * t, 5)] = inverse_yz(t, g_buf, d_far, far_w, y_ref, z_ref)
         e_copy(t).start()
 
@@ -330,8 +345,7 @@
     def _(yt):
         middle_x(yt, d_own, green_ref)
 
-    @pl.loop(0, 3)
-    def _(t):
+    for t in range(3):
         own = inverse_yz(t, g_buf, d_own, own_w, y_ref, z_ref)
         e_copy(t).wait()
         own = own + e_in[pl.ds(5 * t, 5)]
@@ -381,7 +395,7 @@
             pltpu.VMEM((RING - 1, PART, 4, 128), f32),
             pltpu.VMEM((PART, 4, 128), f32),
             dma((2,)), dma((3,)), dma((3,)), dma((2,)), dma((2,)),
-            dma((PLANE - 1,)), dma((PLANE - 1,)), dma((RING - 1,)), dma((RING - 1,)), dma((PLANE - 1,)), dma((PLANE - 1,)),
+            dma, dma, dma, dma, dma, dma,
         ],
         compiler_params=pltpu.CompilerParams(
             collective_id=0, has_side_effects=True, vmem_limit_bytes=48 << 20

time: 54.1 us -> 52.5 us (0.970)
  Pallas kernels: 38.6 us -> 36.9 us
    pallas_call x1, Pallas kernels: 38.6 us -> 36.9 us  [per_device(): pl.pallas_call(kernel, out_shape=(jax.ShapeDtypeStruct((NX, NY, NZ), f32)...]
where the time goes in v1:
time: 52.5 us; the launch traced here: 52.1 us
  Pallas kernels  36.9 us (70%)
  local copies, waits for them, and re-layouts  10.9 us (21%)
  other arithmetic  4.23 us (8%)
    pallas_call x1, Pallas kernels, per_device(): pl.pallas_call(kernel, out_shape=(jax.ShapeDtypeStruct((NX, NY, NZ), f32)...  36.9 us
    reshape x1, local copies, waits for them, and re-layouts, per_device(): ground_orbitals.reshape(NB, NX, NY, NZ)  5.38 us
    dynamic_slice x1, local copies, waits for them, and re-layouts, per_device(): lax.dynamic_slice_in_dim(ground_orbitals, own_start, 1, 0).reshape(points)  2.25 us
    unnamed x1, other arithmetic  1.79 us

profile of v1, /device:TPU:1, one launch (start us, length us, event | category | flops | bytes accessed | tf_op | source)
XLA Modules:
  0.0 52.1 jit_solution(4961587298478603144)
XLA Ops:
  0.0 0.7 %convert_element_type.8 = f32[4]{0:T(128)S(1)} convert(s32[4]{0:T(128)} %param.9) | non-fusion elementwise | flops 4 | bytes 32 | tf_op jit(solution)/shard_map/convert_element_type | solution.py:362
  0.7 0.6 %dynamic_slice.6 = f32[1]{0:T(128)} dynamic-slice(f32[4]{0:T(128)S(1)} %convert_element_type.8, s32[]{:T(128)S(6)} %select_n.4), dynamic_slice_sizes={1} | dynamic-slice | bytes 12 | tf_op jit(solution)/shard_map/dynamic_slice | solution.py:365
  1.2 0.7 %convert_bitcast_fusion = f32[2]{0:T(128)S(1)} fusion(s32[1,2]{1,0:T(1,128)} %param.11), kind=kLoop, calls=%fused_computation.6 | loop fusion | flops 2 | bytes 16 | tf_op jit(solution)/shard_map/broadcast_in_dim | solution.py:370
  1.9 0.1 broadcast_in_dim.15.offsets_ref
  2.0 0.1 broadcast_in_dim.13
  2.0 0.1 broadcast_in_dim_reshape.3.signs_ref
  2.1 2.3 %dynamic-slice_reduce_fusion = f32[81000]{0:T(1024)S(1)} fusion(f32[4,81000]{1,0:T(4,128)} %param.8, s32[]{:T(128)S(6)} %select_n.4), kind=kLoop, calls=%fused_computation.5 | loop fusion | bytes 648004 | tf_op jit(solution)/shard_map/dynamic_slice | solution.py:364
  4.4 1.8 %reduce = f32[81000]{0:T(1024)S(1)} reduce(f32[1,81000]{1,0:T(1,128)} %param.10, f32[]{:T(128)} %constant.31), dimensions={0}, to_apply=%param.10.reduce_sub_computation | reduce | bytes 648004 | tf_op args[2]
  6.2 0.7 %multiply_multiply_fusion = f32[81000]{0:T(1024)S(1)} fusion(f32[81000]{0:T(1024)S(1)} %reduce, f32[81000]{0:T(1024)S(1)} %dynamic-slice_reduce_fusion, f32[]{:T(128)} %bitcast), kind=kLoop, calls=%fused_computation.4 | loop fusion | flops 162000 | bytes 972004 | tf_op jit(solution)/shard_map/mul | solution.py:367
  6.9 0.5 reshape_reshape.3.p_ref
  7.4 0.0 copy-start
  7.4 0.0 copy-start.1
  7.4 0.0 copy-start.2
  7.5 5.4 %reshape.20.g_ref = f32[4,30,45,60]{3,2,1,0:T(8,128)} reshape(f32[4,81000]{1,0:T(4,128)} %param.8) | data formatting | bytes 2592000 | tf_op jit(solution)/shard_map/reshape | solution.py:404
  12.8 0.0 copy-done
  12.8 0.0 copy-done.1
  12.8 0.0 copy-done.2
  12.8 36.9 %shard_map.82 = (f32[30,45,60]{2,1,0:T(8,128)S(1)}, f32[160,4,128]{2,1,0:T(4,128)S(1)}) custom-call(f32[4,30,45,60]{3,2,1,0:T(8,128)} %reshape.20.g_ref, f32[30,45,60]{2,1,0:T(8,128)S(1)} %reshape_reshape.3.p_ref, f32[160,4,128]{2,1,0:T(4,128)S(1)} %bitcast.5, f32[1,256]{1,0:T(1,128)S(1)} %broadcast_in_dim_reshape.3.signs_ref, ...), custom_call_target="tpu_custom_call" | custom-call | tf_op jit(solution)/shard_map/pallas_call | solution.py:375
  49.8 0.0 copy-start.3
  49.8 0.1 broadcast_multiply_fusion
  49.8 0.5 mul.44
  50.4 0.4 copy-done.3
  50.8 0.4 fusion.1
  51.1 0.9 %broadcast_in_dim.16 = f32[1,81000]{1,0:T(1,128)} reshape(f32[81000]{0:T(1024)S(1)} %fusion.1) | data formatting | bytes 648000 | tf_op jit(solution)/shard_map/broadcast_in_dim | solution.py:408
  (1 shorter events, 0.0 us)
Async XLA Ops:
  7.4 5.4 %copy-start = (bf16[2,2,256,256]{3,2,1,0:T(8,128)(2,1)S(1)}, bf16[2,2,256,256]{3,2,1,0:T(8,128)(2,1)}, u32[]{:S(2)}) copy-start(bf16[2,2,256,256]{3,2,1,0:T(8,128)(2,1)} %constant.23.clone.z_ref) | copy-start | bytes 1572868
  7.4 5.4 %copy-start.1 = (bf16[2,2,240,240]{3,2,1,0:T(8,128)(2,1)S(1)}, bf16[2,2,240,240]{3,2,1,0:T(8,128)(2,1)}, u32[]{:S(2)}) copy-start(bf16[2,2,240,240]{3,2,1,0:T(8,128)(2,1)} %constant.22.clone.y_ref) | copy-start | bytes 1382404
  7.4 5.4 %copy-start.2 = (f32[16,48,128]{2,1,0:T(8,128)S(1)}, f32[16,48,128]{2,1,0:T(8,128)}, u32[]{:S(2)}) copy-start(f32[16,48,128]{2,1,0:T(8,128)} %constant.24.clone.green_ref) | copy-start | bytes 1179652
  49.8 1.0 %copy-start.3 = (f32[81000]{0:T(1024)S(1)}, f32[81000]{0:T(1024)}, u32[]{:S(2)}) copy-start(f32[81000]{0:T(1024)} %param.12) | copy-start | bytes 972004

commit v2 on v1

--- a/solution.py
+++ b/solution.py
@@ -178,10 +178,12 @@
 
 
 MESH = pl.DeviceIdType.MESH
-HALF = 80
-PART = 5
-PLANE = 16
+SPOTS = 16
+CHIPS = 32
 RING = 8
+ROWS = 24
+WINDOW = 1920
+TILES = 15
 
 
 def device(orb, grid):
@@ -198,28 +200,45 @@
     pltpu.make_async_copy(ref, ref, sem).wait()
 
 
-def place_response(p_ref, p_buf):
-    @pl.loop(0, XH)
-    def _(i):
-        p_buf[i] = jnp.zeros((YP, 128), jnp.float32)
-        for half in range(2):
-            p_buf[i, 0:NY, ZP * half:ZP * half + NZ] = p_ref[i + XH * half]
-
-
-def place_ground(g_ref, g_buf):
-    @pl.loop(0, XH)
-    def _(i):
-        for half in range(2):
-            g_buf[half, i] = jnp.zeros((YP, 256), jnp.float32)
-            for q in range(NB):
-                g_buf[half, i, 0:NY, ZP * q:ZP * q + NZ] = g_ref[q, i + XH * half]
+def cut_rows(flat, last, rows, points):
+    lane = lax.broadcasted_iota(jnp.int32, (8, 128), 1)
+
+    def cut(base, count, tile):
+        for r in range(count):
+            j, off = divmod(NZ * r, 128)
+            both = tile(j) if off <= 128 - NZ else jnp.where(lane < off, tile(j + 1), tile(j))
+            rows[pl.ds(base + 8 * r, 8), :] = pltpu.roll(both, 128 - off, 1) if off else both
+
+    whole = points // WINDOW
+    tail = points - points // 128 * 128
+    last[...] = jnp.zeros((8, 128), jnp.float32)
+    last[:, 0:tail] = flat[:, points - tail:points]
+
+    @pl.loop(0, whole, unroll=6)
+    def _(k):
+        cut(
+            pl.multiple_of(k * 256, 256), 32,
+            lambda j: flat[:, pl.ds(pl.multiple_of(k * WINDOW + j * 128, 128), 128)],
+        )
+
+    end = whole * TILES
+    cut(
+        whole * 256, (points - whole * WINDOW) // NZ,
+        lambda j: last[...] if end + j == points // 128 else flat[:, (end + j) * 128:(end + j + 1) * 128],
+    )
+    rows[8 * (NX * NY):8 * (NX * NY + YP - NY), :] = jnp.zeros((8 * (YP - NY), 128), jnp.float32)
+
+
+def plane(rows, x, line):
+    return rows[pl.ds(x * (8 * NY) + line, YP, stride=8), :]
 
 
 def kernel(
-    g_ref, p_ref, term_ref, signs_ref, offsets_ref, y_ref, z_ref, green_ref,
-    e_ref, rho_ref,
-    g_buf, p_buf, q_buf, d_own, d_far, e_out, e_in, pair_in, half_sum, plane_in, part_sum, ring_in, part_all,
-    p_sems, e_send, e_recv, pair_sems, swap_sems, plane_send, plane_recv, ring_send, ring_recv, all_send, all_recv,
+    ground_ref, response_ref, density_ref, signs_ref, offsets_ref, y_ref, z_ref, green_ref,
+    out_ref,
+    flat, last, rows, g_buf, p_buf, q_buf, own_buf, d_own, d_far, e_out, e_in,
+    term, pair_in, half_sum, plane_in, part_sum, ring_in, part_all, rho,
+    in_sems, p_sems, e_send, e_recv, pair_sems, plane_send, plane_recv, ring_send, ring_recv, all_send, all_recv,
 ):
     orb, grid = lax.axis_index("orb"), lax.axis_index("grid")
     core = lax.rem(orb, 2)
@@ -230,9 +249,20 @@
     right = device(lax.rem(orb + 1, 64), grid)
     partner = device(orb + 1 - 2 * core, grid)
 
+    loads = (
+        pltpu.make_async_copy(ground_ref, flat.at[0:NB], in_sems.at[0]),
+        pltpu.make_async_copy(response_ref, flat.at[NB:NB + 1], in_sems.at[1]),
+    )
+    for load in loads:
+        load.start()
+
     def in_plane(d):
-        other = lax.rem(spot + d, PLANE)
+        other = lax.rem(spot + d, SPOTS)
         return other, device(other * 4 + lax.rem(orb, 4), grid)
+
+    def in_chips(d):
+        other = lax.rem(spot * 2 + core + d, CHIPS)
+        return device(other // 2 * 4 + z_lo * 2 + lax.rem(other, 2), grid)
 
     def in_ring(d):
         other = lax.rem(level + d, RING)
@@ -243,57 +273,73 @@
     def greet(target):
         pl.semaphore_signal(barrier, inc=1, device_id=target, device_id_type=MESH)
 
-    for target in (left, right, partner):
+    for target in (left, right):
         greet(target)
 
-    @pl.loop(1, PLANE)
+    @pl.loop(1, CHIPS)
     def _(d):
-        greet(in_plane(d)[1])
+        greet(in_chips(d))
 
     @pl.loop(1, RING)
     def _(d):
         greet(in_ring(d))
 
-    place_response(p_ref, p_buf)
-    p_buf[0, NY:YP, :] = jnp.broadcast_to(offsets_ref[1:2, :], (YP - NY, 128))
-    pl.semaphore_wait(barrier, 3 + PLANE - 1 + RING - 1)
+    for load in loads:
+        load.wait()
+    cut_rows(flat, last, rows, flat.shape[1])
+
+    low = lax.broadcasted_iota(jnp.int32, (YP, 128), 1) < ZP
+    own_sign = signs_ref[grid].astype(jnp.float32)
+
+    def packed(i, line):
+        return jnp.where(low, plane(rows, i, line), pltpu.roll(plane(rows, i + XH, line), ZP, 1))
+
+    @pl.loop(0, XH)
+    def _(i):
+        p, own = packed(i, NB), packed(i, grid)
+        p_buf[i] = p
+        own_buf[i] = own
+        term[pl.ds(2 * i, 2)] = (own * own_sign * p).reshape(2, ROWS, 128)
+
+    term[2 * XH:CHIPS] = jnp.zeros((CHIPS - 2 * XH, ROWS, 128), jnp.float32)
+    p_buf[0, NY:YP, :] = jnp.broadcast_to(offsets_ref[0, 1].astype(jnp.float32), (YP - NY, 128))
+    pl.semaphore_wait(barrier, 2 + CHIPS - 1 + RING - 1)
+
+    give_half = remote(term.at[pl.ds((1 - core) * SPOTS, SPOTS)], pair_in, pair_sems.at[0], pair_sems.at[1], partner)
+    give_half.start()
+
+    @pl.loop(0, XH)
+    def _(i):
+        for half in range(2):
+            x = i + XH * half
+            for pair in (0, 2):
+                g = jnp.where(low, plane(rows, x, pair), pltpu.roll(plane(rows, x, pair + 1), ZP, 1))
+                g_buf[half, i, :, 64 * pair:64 * pair + 128] = g
+
+    give_half.wait()
+    half_sum[...] = term[pl.ds(core * SPOTS, SPOTS)] + pair_in[...]
+
+    @pl.loop(1, SPOTS)
+    def _(d):
+        other, target = in_plane(d)
+        remote(half_sum.at[other], plane_in.at[d - 1], plane_send, plane_recv, target).start()
 
     give_p = remote(p_buf, q_buf, p_sems.at[0], p_sems.at[1], left)
     give_p.start()
-    give_half = remote(term_ref.at[pl.ds((1 - core) * HALF, HALF)], pair_in, pair_sems.at[0], pair_sems.at[1], partner)
-    give_half.start()
-    place_ground(g_ref, g_buf)
-    give_half.wait()
-    half_sum[...] = term_ref[pl.ds(core * HALF, HALF)] + pair_in[...]
-
-    def plane_copy(d):
-        other, target = in_plane(d)
-        return remote(half_sum.at[pl.ds(other * PART, PART)], plane_in.at[d - 1], plane_send, plane_recv, target)
-
-    @pl.loop(1, PLANE)
-    def _(d):
-        plane_copy(d).start()
-
-    signs = signs_ref[...]
-    lane_q = (lax.broadcasted_iota(jnp.int32, (1, 256), 1) // ZP).astype(jnp.float32)
 
     for t in range(3):
         forward_yz(t, p_buf, g_buf, d_own, y_ref, z_ref)
 
-    drain(half_sum.at[pl.ds(0, HALF - PART)], plane_send)
+    drain(half_sum.at[pl.ds(0, SPOTS - 1)], plane_send)
     drain(plane_in, plane_recv)
-
-    part = half_sum[pl.ds(spot * PART, PART)]
-    for d in range(PLANE - 1):
+    part = half_sum[spot]
+    for d in range(SPOTS - 1):
         part = part + plane_in[d]
     part_sum[...] = part
 
-    def ring_copy(d):
-        return remote(part_sum, ring_in.at[d - 1], ring_send, ring_recv, in_ring(d))
-
     @pl.loop(1, RING)
     def _(d):
-        ring_copy(d).start()
+        remote(part_sum, ring_in.at[d - 1], ring_send, ring_recv, in_ring(d)).start()
 
     give_p.wait_recv()
 
@@ -302,36 +348,30 @@
 
     drain(ring_in, ring_send)
     drain(ring_in, ring_recv)
-
     part = part_sum[...]
     for d in range(RING - 1):
         part = part + ring_in[d]
     part_all[...] = part
-    mine = pl.ds(core * HALF + spot * PART, PART)
-    rho_ref[mine] = part
-
-    def all_copy(d):
-        return remote(part_all, rho_ref.at[mine], all_send, all_recv, in_plane(d)[1])
-
-    @pl.loop(1, PLANE)
+    mine = core * SPOTS + spot
+    rho[mine] = part
+
+    @pl.loop(1, CHIPS)
     def _(d):
-        all_copy(d).start()
+        remote(part_all, rho.at[mine], all_send, all_recv, in_chips(d)).start()
 
     @pl.loop(0, YP // 8)
     def _(yt):
         middle_x(yt, d_far, green_ref)
 
-    drain(half_sum.at[pl.ds(0, HALF - PART)], all_send)
-    drain(half_sum.at[pl.ds(0, HALF - PART)], all_recv)
-
-    our_half = rho_ref.at[pl.ds(core * HALF, HALF)]
-    swap = remote(our_half, our_half, swap_sems.at[0], swap_sems.at[1], partner)
-    swap.start()
-
+    lane_q = lax.broadcasted_iota(jnp.int32, (1, 256), 1) // ZP
+    signs = jnp.zeros((1, 256), jnp.float32)
+    for q in range(NB):
+        signs = jnp.where(lane_q == q, signs_ref[q].astype(jnp.float32), signs)
+    lane_q = lane_q.astype(jnp.float32)
     far_offset = q_buf[0, NY:NY + 1, :]
     far_w = signs * (lane_q >= jnp.concatenate([far_offset, far_offset], 1)).astype(jnp.float32)
-    own_offset = offsets_ref[0:1, :]
-    own_w = signs * (lane_q >= jnp.concatenate([own_offset, own_offset], 1)).astype(jnp.float32)
+    own_offset = jnp.broadcast_to(offsets_ref[0, 0].astype(jnp.float32), (1, 256))
+    own_w = signs * (lane_q >= own_offset).astype(jnp.float32)
 
     def e_copy(t):
         planes = pl.ds(5 * t, 5)
@@ -341,71 +381,70 @@
         e_out[pl.ds(5 * t, 5)] = inverse_yz(t, g_buf, d_far, far_w, y_ref, z_ref)
         e_copy(t).start()
 
+    @pl.loop(0, XH)
+    def _(i):
+        for half in range(2):
+            p_buf_lanes = pl.ds(ZP * half, NZ)
+            density = density_ref[i + XH * half]
+            scale = jnp.exp(jnp.log(density) * (-2.0 / 3.0)) * -XC_COEF
+            own_buf[i, 0:NY, p_buf_lanes] = own_buf[i, 0:NY, p_buf_lanes] * scale
+
     @pl.loop(0, YP // 8)
     def _(yt):
         middle_x(yt, d_own, green_ref)
 
     for t in range(3):
-        own = inverse_yz(t, g_buf, d_own, own_w, y_ref, z_ref)
+        e_out_t = inverse_yz(t, g_buf, d_own, own_w, y_ref, z_ref)
         e_copy(t).wait()
-        own = own + e_in[pl.ds(5 * t, 5)]
-        for i in range(5):
-            e_ref[5 * t + i] = own[i, :NY, :NZ]
-            e_ref[XH + 5 * t + i] = own[i, :NY, ZP:ZP + NZ]
+        e_in[pl.ds(5 * t, 5)] = (e_out_t + e_in[pl.ds(5 * t, 5)]) * -HYBRID
+
+    drain(rho.at[pl.ds(0, CHIPS - 1)], all_send)
+    drain(rho.at[pl.ds(0, CHIPS - 1)], all_recv)
+
+    @pl.loop(0, XH)
+    def _(i):
+        total = own_buf[i] * rho[pl.ds(2 * i, 2)].reshape(YP, 128) + e_in[i]
+        out_ref[i] = total[:NY, :NZ]
+        out_ref[XH + i] = total[:NY, ZP:ZP + NZ]
 
     give_p.wait_send()
-    swap.wait()
 
 
 def per_device(ground_orbitals, occupation_signs, response_orbitals, window_offsets, ground_density):
     points = response_orbitals.shape[1]
-    signs = occupation_signs.astype(jnp.float32)
-    own_start = lax.axis_index("grid")
-    own_ground = lax.dynamic_slice_in_dim(ground_orbitals, own_start, 1, 0).reshape(points)
-    own_sign = lax.dynamic_slice_in_dim(signs, own_start, 1, 0)
-    response = response_orbitals.reshape(points)
-    term = own_sign * own_ground * response
-    term = jnp.pad(term, (0, 2 * HALF * 512 - points)).reshape(2 * HALF, 4, 128)
-    signs_lanes = jnp.repeat(signs, ZP)[None]
-    offsets = jnp.broadcast_to(window_offsets.astype(jnp.float32).reshape(2, 1), (2, 128))
     y_mats, z_mats, green = tables()
     vmem = pl.BlockSpec(memory_space=pltpu.VMEM)
+    smem = pl.BlockSpec(memory_space=pltpu.SMEM)
+    hbm = pl.BlockSpec(memory_space=pltpu.HBM)
     f32 = jnp.float32
     dma = pltpu.SemaphoreType.DMA
-    exchange, rho = pl.pallas_call(
+    grid_planes = pltpu.VMEM((XH, YP, 128), f32)
+    wide_planes = pltpu.VMEM((2, XH, YP, 256), f32)
+
+    def chunks(*count):
+        return pltpu.VMEM((*count, ROWS, 128), f32)
+
+    action = pl.pallas_call(
         kernel,
-        out_shape=(
-            jax.ShapeDtypeStruct((NX, NY, NZ), f32),
-            jax.ShapeDtypeStruct((2 * HALF, 4, 128), f32),
-        ),
-        in_specs=[vmem] * 8,
-        out_specs=(vmem, vmem),
+        out_shape=jax.ShapeDtypeStruct((NX, NY, NZ), f32),
+        in_specs=[hbm, hbm, vmem, smem, smem, vmem, vmem, vmem],
+        out_specs=vmem,
         scratch_shapes=[
-            pltpu.VMEM((2, XH, YP, 256), f32),
-            pltpu.VMEM((XH, YP, 128), f32),
-            pltpu.VMEM((XH, YP, 128), f32),
-            pltpu.VMEM((2, XH, YP, 256), f32),
-            pltpu.VMEM((2, XH, YP, 256), f32),
-            pltpu.VMEM((XH, YP, 128), f32),
-            pltpu.VMEM((XH, YP, 128), f32),
-            pltpu.VMEM((HALF, 4, 128), f32),
-            pltpu.VMEM((HALF, 4, 128), f32),
-            pltpu.VMEM((PLANE - 1, PART, 4, 128), f32),
-            pltpu.VMEM((PART, 4, 128), f32),
-            pltpu.VMEM((RING - 1, PART, 4, 128), f32),
-            pltpu.VMEM((PART, 4, 128), f32),
-            dma((2,)), dma((3,)), dma((3,)), dma((2,)), dma((2,)),
-            dma, dma, dma, dma, dma, dma,
+            pltpu.VMEM((8, points), f32),
+            pltpu.VMEM((8, 128), f32),
+            pltpu.VMEM((8 * (NX * NY + YP - NY), 128), f32),
+            wide_planes, grid_planes, grid_planes, grid_planes, wide_planes, wide_planes, grid_planes, grid_planes,
+            chunks(CHIPS), chunks(SPOTS), chunks(SPOTS), chunks(SPOTS - 1), chunks(), chunks(RING - 1), chunks(), chunks(CHIPS),
+            dma((2,)), dma((2,)), dma((3,)), dma((3,)), dma((2,)), dma, dma, dma, dma, dma, dma,
         ],
         compiler_params=pltpu.CompilerParams(
-            collective_id=0, has_side_effects=True, vmem_limit_bytes=48 << 20
+            collective_id=0, has_side_effects=True, vmem_limit_bytes=28 << 20
         ),
     )(
-        ground_orbitals.reshape(NB, NX, NY, NZ), response.reshape(NX, NY, NZ),
-        term, signs_lanes, offsets, y_mats, z_mats, green,
+        ground_orbitals, response_orbitals, ground_density.reshape(NX, NY, NZ),
+        occupation_signs, window_offsets, y_mats, z_mats, green,
     )
-    potential = -XC_COEF * ground_density ** (-2.0 / 3.0) * rho.reshape(-1)[:points]
-    return (potential * own_ground - HYBRID * exchange.reshape(points))[None]
+    return action.reshape(1, points)
 
 
 def solution(mesh):

time: 52.5 us -> 46.4 us (0.88)
  other arithmetic: 4.23 us -> 0 us
  local copies, waits for them, and re-layouts: 10.9 us -> 7.61 us
  Pallas kernels: 36.9 us -> 38.5 us
    unnamed x8 -> x14, local copies, waits for them, and re-layouts: 0.41 us -> 4.59 us
    dynamic_slice x2 -> x0, local copies, waits for them, and re-layouts: 2.84 us -> none  [the longest x1 2.25 us: per_device(): lax.dynamic_slice_in_dim(ground_orbitals, own_start, 1, 0).reshape(points)]
    reshape x1 -> x2, local copies, waits for them, and re-layouts: 5.38 us -> 3.02 us  [the longest x1 1.57 us: per_device(): ground_density.reshape(NX, NY, NZ)]
    unnamed x1 -> x0, other arithmetic: 1.79 us -> none
    pallas_call x1, Pallas kernels: 36.9 us -> 38.5 us  [per_device(): pl.pallas_call(kernel, out_shape=jax.ShapeDtypeStruct((NX, NY, NZ), f32),...]
    broadcast_in_dim x3 -> x0, local copies, waits for them, and re-layouts: 1.09 us -> none  [the longest x1 0.95 us: per_device(): return (potential * own_ground - HYBRID * exchange.reshape(points))[None]]
    mul x2 -> x0, other arithmetic: 0.75 us -> none  [the longest x1 0.7 us: per_device(): term = own_sign * own_ground * response]
    broadcast_in_dim x1 -> x0, other arithmetic: 0.66 us -> none  [per_device(): jnp.broadcast_to(window_offsets.astype(jnp.float32).reshape(2, 1), (2, 128))]
where the time goes in v2:
time: 46.4 us; the launch traced here: 46.2 us
  Pallas kernels  38.5 us (83%)
  local copies, waits for them, and re-layouts  7.61 us (16%)
    pallas_call x1, Pallas kernels, per_device(): pl.pallas_call(kernel, out_shape=jax.ShapeDtypeStruct((NX, NY, NZ), f32),...  38.5 us
    unnamed x14, local copies, waits for them, and re-layouts  4.59 us
    reshape x1, local copies, waits for them, and re-layouts, per_device(): ground_density.reshape(NX, NY, NZ)  1.57 us
    reshape x1, local copies, waits for them, and re-layouts, per_device(): return action.reshape(1, points)  1.45 us

profile of v2, /device:TPU:1, one launch (start us, length us, event | category | flops | bytes accessed | tf_op | source)
XLA Modules:
  0.0 46.2 jit_solution(5024768125747768057)
XLA Ops:
  0.0 0.0 copy-start.1
  0.0 0.0 copy-start.2
  0.0 1.6 %reshape.6.density_ref = f32[30,45,60]{2,1,0:T(8,128)S(1)} reshape(f32[81000]{0:T(1024)} %param.12) | data formatting | bytes 648000 | tf_op jit(solution)/shard_map/reshape | solution.py:444
  1.6 0.0 copy-done.1
  1.6 0.0 copy-done.2
  1.6 0.0 copy-start
  1.6 1.3 %copy-done = f32[4,81000]{1,0:T(4,128)S(1)} copy-done((f32[4,81000]{1,0:T(4,128)S(1)}, f32[4,81000]{1,0:T(4,128)}, u32[]{:S(2)}) %copy-start) | copy-done | bytes 1296024
  2.9 0.0 copy-start.3
  2.9 1.0 %copy-done.3 = f32[16,48,128]{2,1,0:T(8,128)S(1)} copy-done((f32[16,48,128]{2,1,0:T(8,128)S(1)}, f32[16,48,128]{2,1,0:T(8,128)}, u32[]{:S(2)}) %copy-start.3) | copy-done | bytes 393240
  3.9 0.0 copy-start.4
  3.9 1.0 %copy-done.4 = f32[1,81000]{1,0:T(1,128)S(1)} copy-done((f32[1,81000]{1,0:T(1,128)S(1)}, f32[1,81000]{1,0:T(1,128)}, u32[]{:S(2)}) %copy-start.4) | copy-done | bytes 324024
  4.9 0.0 copy-start.5
  4.9 0.7 %copy-done.5 = s32[4]{0:T(128)S(1)} copy-done((s32[4]{0:T(128)S(1)}, s32[4]{0:T(128)}, u32[]{:S(2)}) %copy-start.5) | copy-done | bytes 40
  5.5 0.0 copy-start.6
  5.5 0.7 %copy-done.6 = s32[1,2]{1,0:T(1,128)S(1)} copy-done((s32[1,2]{1,0:T(1,128)S(1)}, s32[1,2]{1,0:T(1,128)}, u32[]{:S(2)}) %copy-start.6) | copy-done | bytes 32
  6.2 38.5 %shard_map.82 = f32[30,45,60]{2,1,0:T(8,128)S(1)} custom-call(f32[4,81000]{1,0:T(4,128)S(1)} %copy-done, f32[1,81000]{1,0:T(1,128)S(1)} %copy-done.4, f32[30,45,60]{2,1,0:T(8,128)S(1)} %reshape.6.density_ref, s32[4]{0:T(128)S(1)} %copy-done.5, s32[1,2]{1,0:T(1,128)S(1)} %copy-done.6, bf16[2,2,240,240]{3,2,1,0:T(8,128)(2,1)S(1)} %copy-done.2, ...), custom_call_target="tpu_custom_call" | custom-call | tf_op jit(solution)/shard_map/pallas_call | solution.py:427
  44.7 1.4 %reshape.7 = f32[1,81000]{1,0:T(1,128)} reshape(f32[30,45,60]{2,1,0:T(8,128)S(1)} %shard_map.82) | data formatting | bytes 648000 | tf_op jit(solution)/shard_map/reshape | solution.py:447
Async XLA Ops:
  0.0 1.6 %copy-start.1 = (bf16[2,2,256,256]{3,2,1,0:T(8,128)(2,1)S(1)}, bf16[2,2,256,256]{3,2,1,0:T(8,128)(2,1)}, u32[]{:S(2)}) copy-start(bf16[2,2,256,256]{3,2,1,0:T(8,128)(2,1)} %constant.7.clone.z_ref) | copy-start | bytes 1572868
  0.0 1.6 %copy-start.2 = (bf16[2,2,240,240]{3,2,1,0:T(8,128)(2,1)S(1)}, bf16[2,2,240,240]{3,2,1,0:T(8,128)(2,1)}, u32[]{:S(2)}) copy-start(bf16[2,2,240,240]{3,2,1,0:T(8,128)(2,1)} %constant.6.clone.y_ref) | copy-start | bytes 1382404
  1.6 1.3 %copy-start = (f32[4,81000]{1,0:T(4,128)S(1)}, f32[4,81000]{1,0:T(4,128)}, u32[]{:S(2)}) copy-start(f32[4,81000]{1,0:T(4,128)} %ground_ref.1) | copy-start | bytes 3888004
  2.9 1.0 %copy-start.3 = (f32[16,48,128]{2,1,0:T(8,128)S(1)}, f32[16,48,128]{2,1,0:T(8,128)}, u32[]{:S(2)}) copy-start(f32[16,48,128]{2,1,0:T(8,128)} %constant.8.clone.green_ref) | copy-start | bytes 1179652
  3.9 1.0 %copy-start.4 = (f32[1,81000]{1,0:T(1,128)S(1)}, f32[1,81000]{1,0:T(1,128)}, u32[]{:S(2)}) copy-start(f32[1,81000]{1,0:T(1,128)} %response_ref.1) | copy-start | bytes 972004
  4.9 0.7 %copy-start.5 = (s32[4]{0:T(128)S(1)}, s32[4]{0:T(128)}, u32[]{:S(2)}) copy-start(s32[4]{0:T(128)} %signs_ref.1) | copy-start | bytes 52
  5.5 0.7 %copy-start.6 = (s32[1,2]{1,0:T(1,128)S(1)}, s32[1,2]{1,0:T(1,128)}, u32[]{:S(2)}) copy-start(s32[1,2]{1,0:T(1,128)} %offsets_ref.1) | copy-start | bytes 28

commit v3 on v2

--- a/solution.py
+++ b/solution.py
@@ -234,9 +234,9 @@
 
 
 def kernel(
-    ground_ref, response_ref, density_ref, signs_ref, offsets_ref, y_ref, z_ref, green_ref,
+    ground_ref, response_ref, density_ref, signs_ref, offsets_ref, y_hbm, z_hbm, green_hbm,
     out_ref,
-    flat, last, rows, g_buf, p_buf, q_buf, own_buf, d_own, d_far, e_out, e_in,
+    y_ref, z_ref, green_ref, flat, last, rows, g_buf, p_buf, q_buf, own_buf, d_own, d_far, e_out, e_in,
     term, pair_in, half_sum, plane_in, part_sum, ring_in, part_all, rho,
     in_sems, p_sems, e_send, e_recv, pair_sems, plane_send, plane_recv, ring_send, ring_recv, all_send, all_recv,
 ):
@@ -252,8 +252,14 @@
     loads = (
         pltpu.make_async_copy(ground_ref, flat.at[0:NB], in_sems.at[0]),
         pltpu.make_async_copy(response_ref, flat.at[NB:NB + 1], in_sems.at[1]),
-    )
-    for load in loads:
+        pltpu.make_async_copy(density_ref, flat.at[NB + 1:NB + 2], in_sems.at[2]),
+    )
+    fixed = (
+        pltpu.make_async_copy(y_hbm, y_ref, in_sems.at[3]),
+        pltpu.make_async_copy(z_hbm, z_ref, in_sems.at[4]),
+        pltpu.make_async_copy(green_hbm, green_ref, in_sems.at[5]),
+    )
+    for load in loads + fixed:
         load.start()
 
     def in_plane(d):
@@ -327,6 +333,8 @@
     give_p = remote(p_buf, q_buf, p_sems.at[0], p_sems.at[1], left)
     give_p.start()
 
+    for load in fixed:
+        load.wait()
     for t in range(3):
         forward_yz(t, p_buf, g_buf, d_own, y_ref, z_ref)
 
@@ -383,11 +391,7 @@
 
     @pl.loop(0, XH)
     def _(i):
-        for half in range(2):
-            p_buf_lanes = pl.ds(ZP * half, NZ)
-            density = density_ref[i + XH * half]
-            scale = jnp.exp(jnp.log(density) * (-2.0 / 3.0)) * -XC_COEF
-            own_buf[i, 0:NY, p_buf_lanes] = own_buf[i, 0:NY, p_buf_lanes] * scale
+        own_buf[i] = own_buf[i] * (jnp.exp(jnp.log(packed(i, NB + 1)) * (-2.0 / 3.0)) * -XC_COEF)
 
     @pl.loop(0, YP // 8)
     def _(yt):
@@ -427,21 +431,22 @@
     action = pl.pallas_call(
         kernel,
         out_shape=jax.ShapeDtypeStruct((NX, NY, NZ), f32),
-        in_specs=[hbm, hbm, vmem, smem, smem, vmem, vmem, vmem],
+        in_specs=[hbm, hbm, hbm, smem, smem, hbm, hbm, hbm],
         out_specs=vmem,
         scratch_shapes=[
+            pltpu.VMEM(y_mats.shape, jnp.bfloat16), pltpu.VMEM(z_mats.shape, jnp.bfloat16), pltpu.VMEM(green.shape, f32),
             pltpu.VMEM((8, points), f32),
             pltpu.VMEM((8, 128), f32),
             pltpu.VMEM((8 * (NX * NY + YP - NY), 128), f32),
             wide_planes, grid_planes, grid_planes, grid_planes, wide_planes, wide_planes, grid_planes, grid_planes,
             chunks(CHIPS), chunks(SPOTS), chunks(SPOTS), chunks(SPOTS - 1), chunks(), chunks(RING - 1), chunks(), chunks(CHIPS),
-            dma((2,)), dma((2,)), dma((3,)), dma((3,)), dma((2,)), dma, dma, dma, dma, dma, dma,
+            dma((6,)), dma((2,)), dma((3,)), dma((3,)), dma((2,)), dma, dma, dma, dma, dma, dma,
         ],
         compiler_params=pltpu.CompilerParams(
-            collective_id=0, has_side_effects=True, vmem_limit_bytes=28 << 20
+            collective_id=0, has_side_effects=True, vmem_limit_bytes=57 << 20
         ),
     )(
-        ground_orbitals, response_orbitals, ground_density.reshape(NX, NY, NZ),
+        ground_orbitals, response_orbitals, ground_density.reshape(1, points),
         occupation_signs, window_offsets, y_mats, z_mats, green,
     )
     return action.reshape(1, points)

time: 46.4 us -> 44.2 us (0.953)
  local copies, waits for them, and re-layouts: 7.61 us -> 4.48 us
  Pallas kernels: 38.5 us -> 39.6 us
    unnamed x14 -> x0, local copies, waits for them, and re-layouts: 4.59 us -> none
    reshape x1, local copies, waits for them, and re-layouts: 1.45 us -> 2.57 us  [per_device(): return action.reshape(1, points)]
    pallas_call x1, Pallas kernels: 38.5 us -> 39.6 us  [per_device(): pl.pallas_call(kernel, out_shape=jax.ShapeDtypeStruct((NX, NY, NZ), f32),...]
where the time goes in v3:
time: 44.2 us; the launch traced here: 44.1 us
  Pallas kernels  39.6 us (90%)
  local copies, waits for them, and re-layouts  4.48 us (10%)
    pallas_call x1, Pallas kernels, per_device(): pl.pallas_call(kernel, out_shape=jax.ShapeDtypeStruct((NX, NY, NZ), f32),...  39.6 us
    reshape x1, local copies, waits for them, and re-layouts, per_device(): return action.reshape(1, points)  2.57 us
    reshape x1, local copies, waits for them, and re-layouts, per_device(): ground_density.reshape(1, points)  1.92 us

profile of v3, /device:TPU:1, one launch (start us, length us, event | category | flops | bytes accessed | tf_op | source)
XLA Modules:
  0.0 44.1 jit_solution(4259876095621635659)
XLA Ops:
  0.0 1.9 %reshape.6.density_ref = f32[1,81000]{1,0:T(1,128)} reshape(f32[81000]{0:T(1024)} %param.12) | data formatting | bytes 648000 | tf_op jit(solution)/shard_map/reshape | solution.py:449
  1.9 39.6 %shard_map.82 = f32[30,45,60]{2,1,0:T(8,128)} custom-call(f32[4,81000]{1,0:T(4,128)} %ground_ref.1, f32[1,81000]{1,0:T(1,128)} %response_ref.1, f32[1,81000]{1,0:T(1,128)} %reshape.6.density_ref, s32[4]{0:T(128)} %signs_ref.1, s32[1,2]{1,0:T(1,128)} %offsets_ref.1, bf16[2,2,240,240]{3,2,1,0:T(8,128)(2,1)} %constant.6.clone.y_hbm, ...), custom_call_target="tpu_custom_call" | custom-call | tf_op jit(solution)/shard_map/pallas_call | solution.py:431
  41.5 2.6 %reshape.7 = f32[1,81000]{1,0:T(1,128)} reshape(f32[30,45,60]{2,1,0:T(8,128)} %shard_map.82) | data formatting | bytes 648000 | tf_op jit(solution)/shard_map/reshape | solution.py:452

commit v4 on v3

--- a/solution.py
+++ b/solution.py
@@ -184,6 +184,8 @@
 ROWS = 24
 WINDOW = 1920
 TILES = 15
+PIECES = 3
+UNROLL = 7
 
 
 def device(orb, grid):
@@ -200,7 +202,7 @@
     pltpu.make_async_copy(ref, ref, sem).wait()
 
 
-def cut_rows(flat, last, rows, points):
+def cut_rows(flat, last, rows, points, arrive, greetings):
     lane = lax.broadcasted_iota(jnp.int32, (8, 128), 1)
 
     def cut(base, count, tile):
@@ -211,17 +213,22 @@
 
     whole = points // WINDOW
     tail = points - points // 128 * 128
+    for piece in range(PIECES):
+        arrive(piece)
+
+        @pl.loop(0, whole // PIECES // UNROLL)
+        def _(step):
+            for u in range(UNROLL):
+                k = piece * (whole // PIECES) + step * UNROLL + u
+                greetings[piece](step * UNROLL + u)
+                cut(
+                    pl.multiple_of(k * 256, 256), 32,
+                    lambda j: flat[:, pl.ds(pl.multiple_of(k * WINDOW + j * 128, 128), 128)],
+                )
+
+    end = whole * TILES
     last[...] = jnp.zeros((8, 128), jnp.float32)
     last[:, 0:tail] = flat[:, points - tail:points]
-
-    @pl.loop(0, whole, unroll=6)
-    def _(k):
-        cut(
-            pl.multiple_of(k * 256, 256), 32,
-            lambda j: flat[:, pl.ds(pl.multiple_of(k * WINDOW + j * 128, 128), 128)],
-        )
-
-    end = whole * TILES
     cut(
         whole * 256, (points - whole * WINDOW) // NZ,
         lambda j: last[...] if end + j == points // 128 else flat[:, (end + j) * 128:(end + j + 1) * 128],
@@ -249,17 +256,26 @@
     right = device(lax.rem(orb + 1, 64), grid)
     partner = device(orb + 1 - 2 * core, grid)
 
-    loads = (
-        pltpu.make_async_copy(ground_ref, flat.at[0:NB], in_sems.at[0]),
-        pltpu.make_async_copy(response_ref, flat.at[NB:NB + 1], in_sems.at[1]),
-        pltpu.make_async_copy(density_ref, flat.at[NB + 1:NB + 2], in_sems.at[2]),
-    )
+    points = flat.shape[1]
+    cuts = [piece * (points // WINDOW // PIECES) * WINDOW for piece in range(PIECES)] + [points]
+    lines = ((ground_ref, 0, NB), (response_ref, NB, 1), (density_ref, NB + 1, 1))
+    loads = [
+        [
+            pltpu.make_async_copy(
+                source.at[:, cuts[piece]:cuts[piece + 1]],
+                flat.at[first:first + count, cuts[piece]:cuts[piece + 1]],
+                in_sems.at[piece, at],
+            )
+            for at, (source, first, count) in enumerate(lines)
+        ]
+        for piece in range(PIECES)
+    ]
     fixed = (
-        pltpu.make_async_copy(y_hbm, y_ref, in_sems.at[3]),
-        pltpu.make_async_copy(z_hbm, z_ref, in_sems.at[4]),
-        pltpu.make_async_copy(green_hbm, green_ref, in_sems.at[5]),
-    )
-    for load in loads + fixed:
+        pltpu.make_async_copy(y_hbm, y_ref, in_sems.at[PIECES, 0]),
+        pltpu.make_async_copy(z_hbm, z_ref, in_sems.at[PIECES, 1]),
+        pltpu.make_async_copy(green_hbm, green_ref, in_sems.at[PIECES, 2]),
+    )
+    for load in sum(loads, []) + list(fixed):
         load.start()
 
     def in_plane(d):
@@ -282,7 +298,7 @@
     for target in (left, right):
         greet(target)
 
-    @pl.loop(1, CHIPS)
+    @pl.loop(1, CHIPS - 28)
     def _(d):
         greet(in_chips(d))
 
@@ -290,9 +306,16 @@
     def _(d):
         greet(in_ring(d))
 
-    for load in loads:
-        load.wait()
-    cut_rows(flat, last, rows, flat.shape[1])
+    def arrive(piece):
+        for load in loads[piece]:
+            load.wait()
+
+    greetings = (
+        lambda at: greet(in_chips(CHIPS - 28 + at)),
+        lambda at: greet(in_chips(CHIPS - 14 + at)),
+        lambda at: None,
+    )
+    cut_rows(flat, last, rows, points, arrive, greetings)
 
     low = lax.broadcasted_iota(jnp.int32, (YP, 128), 1) < ZP
     own_sign = signs_ref[grid].astype(jnp.float32)
@@ -313,6 +336,9 @@
 
     give_half = remote(term.at[pl.ds((1 - core) * SPOTS, SPOTS)], pair_in, pair_sems.at[0], pair_sems.at[1], partner)
     give_half.start()
+
+    give_p = remote(p_buf, q_buf, p_sems.at[0], p_sems.at[1], left)
+    give_p.start()
 
     @pl.loop(0, XH)
     def _(i):
@@ -330,13 +356,23 @@
         other, target = in_plane(d)
         remote(half_sum.at[other], plane_in.at[d - 1], plane_send, plane_recv, target).start()
 
-    give_p = remote(p_buf, q_buf, p_sems.at[0], p_sems.at[1], left)
-    give_p.start()
-
     for load in fixed:
         load.wait()
     for t in range(3):
         forward_yz(t, p_buf, g_buf, d_own, y_ref, z_ref)
+
+    @pl.loop(0, YP // 8)
+    def _(yt):
+        middle_x(yt, d_own, green_ref)
+
+    @pl.loop(0, XH)
+    def _(i):
+        own_buf[i] = own_buf[i] * (jnp.exp(jnp.log(packed(i, NB + 1)) * (-2.0 / 3.0)) * -XC_COEF)
+
+    give_p.wait_recv()
+
+    for t in range(3):
+        forward_yz(t, q_buf, g_buf, d_far, y_ref, z_ref)
 
     drain(half_sum.at[pl.ds(0, SPOTS - 1)], plane_send)
     drain(plane_in, plane_recv)
@@ -348,24 +384,6 @@
     @pl.loop(1, RING)
     def _(d):
         remote(part_sum, ring_in.at[d - 1], ring_send, ring_recv, in_ring(d)).start()
-
-    give_p.wait_recv()
-
-    for t in range(3):
-        forward_yz(t, q_buf, g_buf, d_far, y_ref, z_ref)
-
-    drain(ring_in, ring_send)
-    drain(ring_in, ring_recv)
-    part = part_sum[...]
-    for d in range(RING - 1):
-        part = part + ring_in[d]
-    part_all[...] = part
-    mine = core * SPOTS + spot
-    rho[mine] = part
-
-    @pl.loop(1, CHIPS)
-    def _(d):
-        remote(part_all, rho.at[mine], all_send, all_recv, in_chips(d)).start()
 
     @pl.loop(0, YP // 8)
     def _(yt):
@@ -389,13 +407,18 @@
         e_out[pl.ds(5 * t, 5)] = inverse_yz(t, g_buf, d_far, far_w, y_ref, z_ref)
         e_copy(t).start()
 
-    @pl.loop(0, XH)
-    def _(i):
-        own_buf[i] = own_buf[i] * (jnp.exp(jnp.log(packed(i, NB + 1)) * (-2.0 / 3.0)) * -XC_COEF)
-
-    @pl.loop(0, YP // 8)
-    def _(yt):
-        middle_x(yt, d_own, green_ref)
+    drain(ring_in, ring_send)
+    drain(ring_in, ring_recv)
+    part = part_sum[...]
+    for d in range(RING - 1):
+        part = part + ring_in[d]
+    part_all[...] = part
+    mine = core * SPOTS + spot
+    rho[mine] = part
+
+    @pl.loop(1, CHIPS)
+    def _(d):
+        remote(part_all, rho.at[mine], all_send, all_recv, in_chips(d)).start()
 
     for t in range(3):
         e_out_t = inverse_yz(t, g_buf, d_own, own_w, y_ref, z_ref)
@@ -440,7 +463,7 @@
             pltpu.VMEM((8 * (NX * NY + YP - NY), 128), f32),
             wide_planes, grid_planes, grid_planes, grid_planes, wide_planes, wide_planes, grid_planes, grid_planes,
             chunks(CHIPS), chunks(SPOTS), chunks(SPOTS), chunks(SPOTS - 1), chunks(), chunks(RING - 1), chunks(), chunks(CHIPS),
-            dma((6,)), dma((2,)), dma((3,)), dma((3,)), dma((2,)), dma, dma, dma, dma, dma, dma,
+            dma((PIECES + 1, 3)), dma((2,)), dma((3,)), dma((3,)), dma((2,)), dma, dma, dma, dma, dma, dma,
         ],
         compiler_params=pltpu.CompilerParams(
             collective_id=0, has_side_effects=True, vmem_limit_bytes=57 << 20

time: 44.2 us -> 42.9 us (0.971)
  Pallas kernels: 39.6 us -> 38.3 us
    pallas_call x1, Pallas kernels: 39.6 us -> 38.3 us  [per_device(): pl.pallas_call(kernel, out_shape=jax.ShapeDtypeStruct((NX, NY, NZ), f32),...]
where the time goes in v4:
time: 42.9 us; the launch traced here: 42.8 us
  Pallas kernels  38.3 us (89%)
  local copies, waits for them, and re-layouts  4.48 us (10%)
    pallas_call x1, Pallas kernels, per_device(): pl.pallas_call(kernel, out_shape=jax.ShapeDtypeStruct((NX, NY, NZ), f32),...  38.3 us
    reshape x1, local copies, waits for them, and re-layouts, per_device(): return action.reshape(1, points)  2.57 us
    reshape x1, local copies, waits for them, and re-layouts, per_device(): ground_density.reshape(1, points)  1.92 us

profile of v4, /device:TPU:1, one launch (start us, length us, event | category | flops | bytes accessed | tf_op | source)
XLA Modules:
  0.0 42.8 jit_solution(9578139556998677259)
XLA Ops:
  0.0 1.9 %reshape.6.density_ref = f32[1,81000]{1,0:T(1,128)} reshape(f32[81000]{0:T(1024)} %param.12) | data formatting | bytes 648000 | tf_op jit(solution)/shard_map/reshape | solution.py:472
  1.9 38.3 %shard_map.82 = f32[30,45,60]{2,1,0:T(8,128)} custom-call(f32[4,81000]{1,0:T(4,128)} %ground_ref.1, f32[1,81000]{1,0:T(1,128)} %response_ref.1, f32[1,81000]{1,0:T(1,128)} %reshape.6.density_ref, s32[4]{0:T(128)} %signs_ref.1, s32[1,2]{1,0:T(1,128)} %offsets_ref.1, bf16[2,2,240,240]{3,2,1,0:T(8,128)(2,1)} %constant.6.clone.y_hbm, ...), custom_call_target="tpu_custom_call" | custom-call | tf_op jit(solution)/shard_map/pallas_call | solution.py:454
  40.2 2.6 %reshape.7 = f32[1,81000]{1,0:T(1,128)} reshape(f32[30,45,60]{2,1,0:T(8,128)} %shard_map.82) | data formatting | bytes 648000 | tf_op jit(solution)/shard_map/reshape | solution.py:475

commit v5 on v4

--- a/solution.py
+++ b/solution.py
@@ -236,6 +236,24 @@
     rows[8 * (NX * NY):8 * (NX * NY + YP - NY), :] = jnp.zeros((8 * (YP - NY), 128), jnp.float32)
 
 
+def join_rows(lines, flat):
+    lane = lax.broadcasted_iota(jnp.int32, (8, 128), 1)
+
+    @pl.loop(0, flat.shape[0] // (8 * TILES))
+    def _(m):
+        turned = []
+        for r in range(32):
+            line = lines[pl.ds(256 * m + r, 8, stride=32), :]
+            off = NZ * r % 128
+            turned.append(pltpu.roll(line, off, 1) if off else line)
+        for t in range(TILES):
+            pieces = [r for r in range(32) if NZ * r < 128 * (t + 1) and NZ * (r + 1) > 128 * t]
+            tile = turned[pieces[0]]
+            for r in pieces[1:]:
+                tile = jnp.where(lane >= NZ * r - 128 * t, turned[r], tile)
+            flat[pl.ds(8 * TILES * m + t, 8, stride=TILES), :] = tile
+
+
 def plane(rows, x, line):
     return rows[pl.ds(x * (8 * NY) + line, YP, stride=8), :]
 
@@ -243,9 +261,9 @@
 def kernel(
     ground_ref, response_ref, density_ref, signs_ref, offsets_ref, y_hbm, z_hbm, green_hbm,
     out_ref,
-    y_ref, z_ref, green_ref, flat, last, rows, g_buf, p_buf, q_buf, own_buf, d_own, d_far, e_out, e_in,
-    term, pair_in, half_sum, plane_in, part_sum, ring_in, part_all, rho,
-    in_sems, p_sems, e_send, e_recv, pair_sems, plane_send, plane_recv, ring_send, ring_recv, all_send, all_recv,
+    y_ref, z_ref, green_ref, flat, last, rows, g_buf, p_buf, q_buf, own_buf, d_own, d_far, e_out, e_in, e_own,
+    lines_out, term, pair_in, half_sum, plane_in, part_sum, ring_in, part_all, rho,
+    in_sems, p_sems, e_send, e_recv, pair_sems, plane_send, plane_recv, ring_send, ring_recv, all_send, all_recv, swap_sems,
 ):
     orb, grid = lax.axis_index("orb"), lax.axis_index("grid")
     core = lax.rem(orb, 2)
@@ -262,8 +280,8 @@
     loads = [
         [
             pltpu.make_async_copy(
-                source.at[:, cuts[piece]:cuts[piece + 1]],
-                flat.at[first:first + count, cuts[piece]:cuts[piece + 1]],
+                source.at[:, cuts[piece]:cuts[piece + 1]] if at < 2 else source.at[cuts[piece]:cuts[piece + 1]],
+                flat.at[first:first + count, cuts[piece]:cuts[piece + 1]] if at < 2 else flat.at[first, cuts[piece]:cuts[piece + 1]],
                 in_sems.at[piece, at],
             )
             for at, (source, first, count) in enumerate(lines)
@@ -416,23 +434,29 @@
     mine = core * SPOTS + spot
     rho[mine] = part
 
-    @pl.loop(1, CHIPS)
+    @pl.loop(1, SPOTS)
     def _(d):
-        remote(part_all, rho.at[mine], all_send, all_recv, in_chips(d)).start()
+        remote(part_all, rho.at[mine], all_send, all_recv, in_plane(d)[1]).start()
 
     for t in range(3):
-        e_out_t = inverse_yz(t, g_buf, d_own, own_w, y_ref, z_ref)
+        if t == 2:
+            drain(rho.at[pl.ds(0, SPOTS - 1)], all_send)
+            drain(rho.at[pl.ds(0, SPOTS - 1)], all_recv)
+            our_half = rho.at[pl.ds(core * SPOTS, SPOTS)]
+            swap = remote(our_half, our_half, swap_sems.at[0], swap_sems.at[1], partner)
+            swap.start()
+        planes = pl.ds(5 * t, 5)
+        e_own[planes] = inverse_yz(t, g_buf, d_own, own_w, y_ref, z_ref)
+    for t in range(3):
         e_copy(t).wait()
-        e_in[pl.ds(5 * t, 5)] = (e_out_t + e_in[pl.ds(5 * t, 5)]) * -HYBRID
-
-    drain(rho.at[pl.ds(0, CHIPS - 1)], all_send)
-    drain(rho.at[pl.ds(0, CHIPS - 1)], all_recv)
-
-    @pl.loop(0, XH)
-    def _(i):
-        total = own_buf[i] * rho[pl.ds(2 * i, 2)].reshape(YP, 128) + e_in[i]
-        out_ref[i] = total[:NY, :NZ]
-        out_ref[XH + i] = total[:NY, ZP:ZP + NZ]
+
+    swap.wait()
+
+    for x in range(NX):
+        i, half = x % XH, x // XH
+        total = own_buf[i] * rho[pl.ds(2 * i, 2)].reshape(YP, 128) + (e_own[i] + e_in[i]) * -HYBRID
+        lines_out[NY * x:NY * x + YP, :] = pltpu.roll(total, ZP, 1) if half else total
+    join_rows(lines_out, out_ref)
 
     give_p.wait_send()
 
@@ -453,7 +477,7 @@
 
     action = pl.pallas_call(
         kernel,
-        out_shape=jax.ShapeDtypeStruct((NX, NY, NZ), f32),
+        out_shape=jax.ShapeDtypeStruct((6 * 8 * TILES, 128), f32),
         in_specs=[hbm, hbm, hbm, smem, smem, hbm, hbm, hbm],
         out_specs=vmem,
         scratch_shapes=[
@@ -461,18 +485,19 @@
             pltpu.VMEM((8, points), f32),
             pltpu.VMEM((8, 128), f32),
             pltpu.VMEM((8 * (NX * NY + YP - NY), 128), f32),
-            wide_planes, grid_planes, grid_planes, grid_planes, wide_planes, wide_planes, grid_planes, grid_planes,
+            wide_planes, grid_planes, grid_planes, grid_planes, wide_planes, wide_planes, grid_planes, grid_planes, grid_planes,
+            pltpu.VMEM((6 * 256, 128), f32),
             chunks(CHIPS), chunks(SPOTS), chunks(SPOTS), chunks(SPOTS - 1), chunks(), chunks(RING - 1), chunks(), chunks(CHIPS),
-            dma((PIECES + 1, 3)), dma((2,)), dma((3,)), dma((3,)), dma((2,)), dma, dma, dma, dma, dma, dma,
+            dma((PIECES + 1, 3)), dma((2,)), dma((3,)), dma((3,)), dma((2,)), dma, dma, dma, dma, dma, dma, dma((2,)),
         ],
         compiler_params=pltpu.CompilerParams(
             collective_id=0, has_side_effects=True, vmem_limit_bytes=57 << 20
         ),
     )(
-        ground_orbitals, response_orbitals, ground_density.reshape(1, points),
+        ground_orbitals, response_orbitals, ground_density,
         occupation_signs, window_offsets, y_mats, z_mats, green,
     )
-    return action.reshape(1, points)
+    return action.reshape(1, -1)[:, :points]
 
 
 def solution(mesh):

time: 42.9 us -> 39.5 us (0.921)
  local copies, waits for them, and re-layouts: 4.48 us -> 1.72 us
  Pallas kernels: 38.3 us -> 37.7 us
    reshape x2 -> x0, local copies, waits for them, and re-layouts: 4.48 us -> none  [the longest x1 2.57 us: per_device(): return action.reshape(1, points)]
    slice x0 -> x1, local copies, waits for them, and re-layouts: none -> 1.72 us  [per_device(): return action.reshape(1, -1)[:, :points]]
    pallas_call x1, Pallas kernels: 38.3 us -> 37.7 us  [per_device(): pl.pallas_call(kernel, out_shape=jax.ShapeDtypeStruct((6 * 8 * TILES, 128...]
where the time goes in v5:
time: 39.5 us; the launch traced here: 39.4 us
  Pallas kernels  37.7 us (95%)
  local copies, waits for them, and re-layouts  1.72 us (4%)
    pallas_call x1, Pallas kernels, per_device(): pl.pallas_call(kernel, out_shape=jax.ShapeDtypeStruct((6 * 8 * TILES, 128...  37.7 us
    slice x1, local copies, waits for them, and re-layouts, per_device(): return action.reshape(1, -1)[:, :points]  1.72 us

profile of v5, /device:TPU:1, one launch (start us, length us, event | category | flops | bytes accessed | tf_op | source)
XLA Modules:
  0.0 39.4 jit_solution(9274592595586929656)
XLA Ops:
  0.0 37.7 %shard_map.82 = f32[720,128]{1,0:T(8,128)} custom-call(f32[4,81000]{1,0:T(4,128)} %ground_ref.1, f32[1,81000]{1,0:T(1,128)} %response_ref.1, f32[81000]{0:T(1024)} %density_ref.1, s32[4]{0:T(128)} %signs_ref.1, s32[1,2]{1,0:T(1,128)} %offsets_ref.1, bf16[2,2,240,240]{3,2,1,0:T(8,128)(2,1)} %constant.6.clone.y_hbm, ...), custom_call_target="tpu_custom_call" | custom-call | tf_op jit(solution)/shard_map/pallas_call | solution.py:478
  37.7 1.7 %slice.4 = f32[1,81000]{1,0:T(1,128)} slice(f32[1,92160]{1,0:T(1,128)} %bitcast.1), slice={[0:1], [0:81000]} | slice | bytes 648000 | tf_op jit(solution)/shard_map/slice | solution.py:500

commit v6 on v5

--- a/solution.py
+++ b/solution.py
@@ -491,11 +491,12 @@
             dma((PIECES + 1, 3)), dma((2,)), dma((3,)), dma((3,)), dma((2,)), dma, dma, dma, dma, dma, dma, dma((2,)),
         ],
         compiler_params=pltpu.CompilerParams(
-            collective_id=0, has_side_effects=True, vmem_limit_bytes=57 << 20
+            collective_id=0, has_side_effects=True, vmem_limit_bytes=40 << 20
         ),
     )(
-        ground_orbitals, response_orbitals, ground_density,
-        occupation_signs, window_offsets, y_mats, z_mats, green,
+        *(pltpu.with_memory_space_constraint(x, pltpu.HBM) for x in (ground_orbitals, response_orbitals, ground_density)),
+        *(pltpu.with_memory_space_constraint(x, pltpu.HBM) for x in (occupation_signs, window_offsets)),
+        *(pltpu.with_memory_space_constraint(jnp.asarray(x), pltpu.HBM) for x in (y_mats, z_mats, green)),
     )
     return action.reshape(1, -1)[:, :points]
 

time: 39.5 us -> 37.8 us (0.957)
  local copies, waits for them, and re-layouts: 1.72 us -> 0.75 us
  Pallas kernels: 37.7 us -> 37 us
    slice x1, local copies, waits for them, and re-layouts: 1.72 us -> 0.75 us  [per_device(): return action.reshape(1, -1)[:, :points]]
    pallas_call x1, Pallas kernels: 37.7 us -> 37 us  [per_device(): pl.pallas_call(kernel, out_shape=jax.ShapeDtypeStruct((6 * 8 * TILES, 128...]
where the time goes in v6:
time: 37.8 us; the launch traced here: 37.7 us
  Pallas kernels  37 us (98%)
  local copies, waits for them, and re-layouts  0.75 us (2%)
    pallas_call x1, Pallas kernels, per_device(): pl.pallas_call(kernel, out_shape=jax.ShapeDtypeStruct((6 * 8 * TILES, 128...  37 us

profile of v6, /device:TPU:1, one launch (start us, length us, event | category | flops | bytes accessed | tf_op | source)
XLA Modules:
  0.0 37.7 jit_solution(7118911387641534368)
XLA Ops:
  0.0 37.0 %shard_map.82 = f32[720,128]{1,0:T(8,128)S(1)} custom-call(f32[4,81000]{1,0:T(4,128)} %ground_ref.1, f32[1,81000]{1,0:T(1,128)} %response_ref.1, f32[81000]{0:T(1024)} %density_ref.1, s32[4]{0:T(128)} %signs_ref.1, s32[1,2]{1,0:T(1,128)} %offsets_ref.1, bf16[2,2,240,240]{3,2,1,0:T(8,128)(2,1)} %constant.6.clone.y_hbm, ...), custom_call_target="tpu_custom_call" | custom-call | tf_op jit(solution)/shard_map/pallas_call | solution.py:478
  37.0 0.7 %slice.4 = f32[1,81000]{1,0:T(1,128)} slice(f32[1,92160]{1,0:T(1,128)S(1)} %bitcast.1), slice={[0:1], [0:81000]} | slice | bytes 648000 | tf_op jit(solution)/shard_map/slice | solution.py:501

commit v7 on v6

--- a/solution.py
+++ b/solution.py
@@ -239,8 +239,9 @@
 def join_rows(lines, flat):
     lane = lax.broadcasted_iota(jnp.int32, (8, 128), 1)
 
-    @pl.loop(0, flat.shape[0] // (8 * TILES))
-    def _(m):
+    points = flat.shape[1]
+
+    def join(m, whole):
         turned = []
         for r in range(32):
             line = lines[pl.ds(256 * m + r, 8, stride=32), :]
@@ -251,7 +252,21 @@
             tile = turned[pieces[0]]
             for r in pieces[1:]:
                 tile = jnp.where(lane >= NZ * r - 128 * t, turned[r], tile)
-            flat[pl.ds(8 * TILES * m + t, 8, stride=TILES), :] = tile
+            for group in range(8):
+                at = (8 * m + group) * WINDOW + 128 * t
+                if whole:
+                    flat[:, pl.ds(pl.multiple_of(at, 128), 128)] = tile[group:group + 1]
+                elif at < points:
+                    width = min(128, points - at)
+                    flat[:, at:at + width] = tile[group:group + 1, :width]
+
+    full = points // (8 * WINDOW)
+
+    @pl.loop(0, full)
+    def _(m):
+        join(m, True)
+
+    join(full, False)
 
 
 def plane(rows, x, line):
@@ -477,7 +492,7 @@
 
     action = pl.pallas_call(
         kernel,
-        out_shape=jax.ShapeDtypeStruct((6 * 8 * TILES, 128), f32),
+        out_shape=jax.ShapeDtypeStruct((1, points), f32),
         in_specs=[hbm, hbm, hbm, smem, smem, hbm, hbm, hbm],
         out_specs=vmem,
         scratch_shapes=[
@@ -498,7 +513,7 @@
         *(pltpu.with_memory_space_constraint(x, pltpu.HBM) for x in (occupation_signs, window_offsets)),
         *(pltpu.with_memory_space_constraint(jnp.asarray(x), pltpu.HBM) for x in (y_mats, z_mats, green)),
     )
-    return action.reshape(1, -1)[:, :points]
+    return action
 
 
 def solution(mesh):

time: 37.8 us -> 38.2 us (1.011)
    slice x1 -> x0, local copies, waits for them, and re-layouts: 0.75 us -> none  [per_device(): return action.reshape(1, -1)[:, :points]]
    unnamed x0 -> x1, local copies, waits for them, and re-layouts: none -> 0.73 us
where the time goes in v7:
time: 38.2 us; the launch traced here: 38.1 us
  Pallas kernels  37.3 us (98%)
  local copies, waits for them, and re-layouts  0.73 us (2%)
    pallas_call x1, Pallas kernels, per_device(): pl.pallas_call(kernel, out_shape=jax.ShapeDtypeStruct((1, points), f32),...  37.3 us

profile of v7, /device:TPU:1, one launch (start us, length us, event | category | flops | bytes accessed | tf_op | source)
XLA Modules:
  0.0 38.1 jit_solution(8795738904443135177)
XLA Ops:
  0.0 37.3 %shard_map.82 = f32[1,81000]{1,0:T(1,128)S(1)} custom-call(f32[4,81000]{1,0:T(4,128)} %ground_ref.1, f32[1,81000]{1,0:T(1,128)} %response_ref.1, f32[81000]{0:T(1024)} %density_ref.1, s32[4]{0:T(128)} %signs_ref.1, s32[1,2]{1,0:T(1,128)} %offsets_ref.1, bf16[2,2,240,240]{3,2,1,0:T(8,128)(2,1)} %constant.6.clone.y_hbm, ...), custom_call_target="tpu_custom_call" | custom-call | tf_op jit(solution)/shard_map/pallas_call | solution.py:493
  37.3 0.7 %copy.10 = f32[1,81000]{1,0:T(1,128)} copy(f32[1,81000]{1,0:T(1,128)S(1)} %shard_map.82) | data formatting | bytes 648000
